TPU v7x, 32 devices: a whole 2x2x4 slice. The times are simulated.
32 devices in a mesh: src: 4 (over z), dst: 8 (over y, x, core).
Axes of the slice: x: 2, y: 2, z: 4, core: 2. Of those that a mesh axis runs over, the one named last changes fastest.
Arguments:
- src_emb: bfloat16 [65536, 128], P('src'), may hold values from -1.5 to 1.5
- dst_emb: bfloat16 [65536, 128], P('dst'), may hold values from -1.5 to 1.5
- out_emb: bfloat16 [65536, 128], P('dst'), may hold values from -1.5 to 1.5
- word_table: bfloat16 [32768, 128], P('dst'), may hold values from -1.5 to 1.5
- log_norm: float32 [65536], P('dst'), may hold values from 9 to 11
- block_mask: int32 [128, 128], P('src', 'dst'), may hold values from 0 to 1, as said below
- tokens: int32 [3, 8], replicated, may hold values from 0 to 32767
- alpha_start: float32 [8, 65536], P(None, 'src'), may hold values from 0.5 to 80
- beta_end: float32 [8, 65536], P(None, 'dst'), may hold values from 0.5 to 80
Outputs:
- alpha_end: float32 [8, 65536], P(None, 'dst')
- beta_start: float32 [8, 65536], P(None, 'src')
- block_counts: float32 [128, 128], P('src', 'dst')
Inputs may be any that keep to these rules, and one draw needn't show every extreme that they name: block_mask[I, I] = 1 for every block I: a state may always move within its own block.
All inputs are finite; a program needn't handle non-finite values.
Results may differ from a plain program's by a relative error of at most 0.0032.
Values may be sent and summed in bfloat16 or wider, within the bound.
A program may use at most 384 MiB of HBM per device.

v0:
```python
import functools

import jax
import jax.numpy as jnp
from jax import lax
from jax.experimental import pallas as pl
from jax.experimental.pallas import tpu as pltpu
from jax.sharding import PartitionSpec as P

BLK = 512
STEPS = 3
NB = 128
LANES = 128
DEPTH = 8
very_negative = -1e30
VMEM_BYTES = 60 * 1024 * 1024


def table_kernel(unit, cols, ids, count, src, dst, top, mass, transit, buf, sems):
    number = count[0]
    chunk = min(256, unit)

    def copy(slot, b):
        return pltpu.make_async_copy(buf.at[b], transit.at[slot], sems.at[b])

    def body(slot, carry):
        b = lax.rem(slot, 2)
        entry = ids[slot]
        i = lax.div(entry, cols)
        j = lax.rem(entry, cols)

        @pl.when(slot >= 2)
        def _():
            copy(slot - 2, b).wait()

        d = dst[pl.ds(pl.multiple_of(j * BLK, BLK), BLK), :]
        for c in range(unit // chunk):
            base = pl.multiple_of(i * unit + c * chunk, chunk)
            scores = lax.dot_general(
                d, src[pl.ds(base, chunk), :], (((1,), (1,)), ((), ())),
                preferred_element_type=jnp.float32,
            )
            best = jnp.max(scores, axis=0, keepdims=True)
            risen = jnp.exp(scores - best)
            buf[b, :, c * chunk:(c + 1) * chunk] = risen.astype(jnp.bfloat16)
            top[pl.ds(j, 1), pl.ds(base, chunk)] = best
            mass[pl.ds(j, 1), pl.ds(base, chunk)] = jnp.sum(risen, axis=0, keepdims=True)
        copy(slot, b).start()
        return carry

    lax.fori_loop(0, number, body, 0)
    for back in (2, 1):

        @pl.when(number >= back)
        def _():
            copy(number - back, lax.rem(number - back, 2)).wait()


def sweep_kernel(unit, cols, traces, kind, ids, count, *refs):
    if kind == 2:
        alpha, early, factor, weight, transit, pred, carried, terms, buf, sems = refs
    elif kind == 1:
        alpha, factor, weight, transit, pred, carried, terms, buf, sems = refs
    else:
        alpha, factor, weight, transit, pred, carried, buf, sems = refs
    number = count[0]
    pred[...] = jnp.zeros_like(pred)
    carried[...] = jnp.zeros_like(carried)
    if kind:
        terms[...] = jnp.zeros_like(terms)

    def copy(slot, b):
        return pltpu.make_async_copy(transit.at[slot], buf.at[b], sems.at[b])

    for p in range(DEPTH):

        @pl.when(p < number)
        def _():
            copy(p, p).start()

    def body(slot, carry):
        b = lax.rem(slot, DEPTH)
        entry = ids[slot]
        i = lax.div(entry, cols)
        j = lax.rem(entry, cols)
        rows = pl.ds(pl.multiple_of(i * unit, unit), unit)
        places = pl.ds(pl.multiple_of(j * BLK, BLK), BLK)
        share = factor[pl.ds(j, 1), rows]
        mix = (alpha[:, rows] * share).astype(jnp.bfloat16)
        w = weight[:, places].astype(jnp.bfloat16)
        copy(slot, b).wait()
        pred[:, places] += lax.dot_general(
            mix, buf[b], (((1,), (1,)), ((), ())), preferred_element_type=jnp.float32
        )
        spread = jnp.dot(w, buf[b], preferred_element_type=jnp.float32)
        carried[:, rows] += share * spread[:traces]

        @pl.when(slot + DEPTH < number)
        def _():
            copy(slot + DEPTH, b).start()

        if kind:
            group = pl.ds(pl.multiple_of(lax.div(entry, LANES) * LANES, LANES), LANES)
            hit = lax.broadcasted_iota(jnp.int32, (traces, LANES), 1) == lax.rem(entry, LANES)

            def note(t, m, s):
                value = jnp.sum(m.astype(jnp.float32) * s, axis=1, keepdims=True)
                terms[t, :, group] += jnp.where(hit, value, 0.0)

            if kind == 1:
                note(0, mix, spread)
            else:
                first = (early[:, rows] * share).astype(jnp.bfloat16)
                note(0, first, spread[:traces])
                note(1, mix, spread[traces:])
        return carry

    lax.fori_loop(0, number, body, 0)


def exchange_kernel(
    lines, piece, states, ahead, behind, glow, alpha, beta,
    in_f, in_b, red_f, red_b, land_f, land_b, send_1, recv_1, send_2, recv_2,
):
    place = {name: lax.axis_index(name) for name in lines}
    mesh_ids = pl.DeviceIdType.MESH

    def peer(name, k):
        return lax.rem(place[name] + k, lines[name])

    def origin(name, k):
        return lax.rem(place[name] + lines[name] - k, lines[name])

    barrier = pltpu.get_barrier_semaphore()
    for name in lines:
        for k in range(1, lines[name]):
            pl.semaphore_signal(
                barrier, inc=1, device_id={name: peer(name, k)}, device_id_type=mesh_ids
            )
    pl.semaphore_wait(barrier, sum(lines.values()) - len(lines))

    offset = {"src": 0, "dst": lines["src"]}
    payload = {"src": ahead, "dst": behind}
    landing = {"src": in_f, "dst": in_b}
    first = {"src": [], "dst": []}
    for name in lines:
        for k in range(1, lines[name]):
            copy = pltpu.make_async_remote_copy(
                src_ref=payload[name].at[peer(name, k)],
                dst_ref=landing[name].at[k],
                send_sem=send_1.at[offset[name] + k],
                recv_sem=recv_1.at[offset[name] + k],
                device_id={name: peer(name, k)},
                device_id_type=mesh_ids,
            )
            copy.start()
            first[name].append(copy)
    second = []
    for name, other, red, land in (("src", "dst", red_f, land_f), ("dst", "src", red_b, land_b)):
        value = payload[name][place[name]]
        for k in range(1, lines[name]):
            first[name][k - 1].wait_recv()
            value = value + landing[name][k]
        if name == "src":
            value = jnp.concatenate([value[:, :piece] * glow[...], value[:, piece:]], axis=1)
        red[...] = value
        for k in range(1, lines[other]):
            copy = pltpu.make_async_remote_copy(
                src_ref=red,
                dst_ref=land.at[k],
                send_sem=send_2.at[offset[other] + k],
                recv_sem=recv_2.at[offset[other] + k],
                device_id={other: peer(other, k)},
                device_id_type=mesh_ids,
            )
            copy.start()
            second.append(copy)
    for copy in second:
        copy.wait_recv()
    for other, red, land, out in (("dst", red_f, land_f, alpha), ("src", red_b, land_b, beta)):
        total = red[:, piece:piece + 1]
        for k in range(1, lines[other]):
            total = total + land[k, :, piece:piece + 1]
        scale = total / states
        for k in range(lines[other]):
            part = red[:, :piece] if k == 0 else land[k, :, :piece]
            start = pl.multiple_of(origin(other, k) * piece, piece)
            out[:, pl.ds(start, piece)] = part / scale
    for copies in (first["src"], first["dst"], second):
        for copy in copies:
            copy.wait_send()


def total_kernel(lines, value, out, red, land_1, land_2, send_1, recv_1, send_2, recv_2):
    place = {name: lax.axis_index(name) for name in lines}
    mesh_ids = pl.DeviceIdType.MESH

    def peer(name, k):
        return lax.rem(place[name] + k, lines[name])

    barrier = pltpu.get_barrier_semaphore()
    for name in lines:
        for k in range(1, lines[name]):
            pl.semaphore_signal(
                barrier, inc=1, device_id={name: peer(name, k)}, device_id_type=mesh_ids
            )
    pl.semaphore_wait(barrier, sum(lines.values()) - len(lines))

    def line_sum(name, given, land, send, recv):
        copies = []
        for k in range(1, lines[name]):
            copy = pltpu.make_async_remote_copy(
                src_ref=given,
                dst_ref=land.at[k],
                send_sem=send.at[k],
                recv_sem=recv.at[k],
                device_id={name: peer(name, k)},
                device_id_type=mesh_ids,
            )
            copy.start()
            copies.append(copy)
        total = given[...]
        for k in range(1, lines[name]):
            copies[k - 1].wait_recv()
            total = total + land[k]
        return total, copies

    red[...], early = line_sum("src", value, land_1, send_1, recv_1)
    out[...], late = line_sum("dst", red, land_2, send_2, recv_2)
    for copy in early + late:
        copy.wait_send()


def local(
    src_emb, dst_emb, out_emb, word_table, log_norm, block_mask, tokens, alpha_start, beta_end
):
    row_count, emb_width = src_emb.shape
    col_count = dst_emb.shape[0]
    traces = alpha_start.shape[0]
    src_count = lax.axis_size("src")
    dst_count = lax.axis_size("dst")
    states = row_count * src_count
    group = dst_count // src_count
    piece = col_count // src_count
    unit = min(BLK, piece)
    units = row_count // unit
    cols = col_count // BLK
    places = units * cols
    padded = -(-places // LANES) * LANES
    src_place = lax.axis_index("src")
    dst_place = lax.axis_index("dst")
    both = ("src", "dst")
    moves = [
        ((d // group) * dst_count + (d % group) * src_count + z, z * dst_count + d)
        for z in range(src_count)
        for d in range(dst_count)
    ]

    def spread_rows(mine):
        moved = lax.ppermute(mine, both, moves)
        return lax.all_gather(moved, "dst", axis=0, tiled=True)

    mine = lax.dynamic_slice_in_dim(src_emb, dst_place * piece, piece, 0)
    src_rows = spread_rows(mine)
    alpha_piece = lax.dynamic_slice_in_dim(alpha_start, dst_place * piece, piece, 1)
    alpha_moved = lax.ppermute(alpha_piece, both, moves)
    alpha_rows = lax.all_gather(alpha_moved, "dst", axis=1, tiled=True)

    whole_mask = lax.all_gather(block_mask, "src", axis=0, tiled=True)
    unit_index = jnp.arange(units, dtype=jnp.int32)
    per_piece = piece // unit
    unit_state = (
        (unit_index // per_piece) * col_count + src_place * piece + (unit_index % per_piece) * unit
    )
    unit_block = unit_state // BLK
    owner = unit_block[:, None] == jnp.arange(whole_mask.shape[0], dtype=jnp.int32)[None, :]
    mask = jnp.sum(jnp.where(owner[:, :, None], whole_mask[None], 0), axis=1)
    flat = (mask == 1).reshape(places)
    index = jnp.arange(places, dtype=jnp.int32)
    before = jnp.sum(
        jnp.where((index[None, :] < index[:, None]) & flat[None, :], 1, 0), axis=1
    )
    ids = jnp.sum(
        jnp.where((before[None, :] == index[:, None]) & flat[None, :], index[None, :], 0), axis=1
    ).astype(jnp.int32)
    number = jnp.sum(flat.astype(jnp.int32)).reshape(1)

    smem = pl.BlockSpec(memory_space=pltpu.SMEM)
    vmem = pl.BlockSpec(memory_space=pltpu.VMEM)
    anywhere = pl.BlockSpec(memory_space=pl.ANY)
    guess = places // 5 + 1
    params = pltpu.CompilerParams(vmem_limit_bytes=VMEM_BYTES)
    top, mass, transit = pl.pallas_call(
        functools.partial(table_kernel, unit, cols),
        out_shape=(
            jax.ShapeDtypeStruct((cols, row_count), jnp.float32),
            jax.ShapeDtypeStruct((cols, row_count), jnp.float32),
            jax.ShapeDtypeStruct((places, BLK, unit), jnp.bfloat16),
        ),
        in_specs=[smem, smem, vmem, vmem],
        out_specs=(vmem, vmem, anywhere),
        scratch_shapes=[
            pltpu.VMEM((2, BLK, unit), jnp.bfloat16),
            pltpu.SemaphoreType.DMA((2,)),
        ],
        compiler_params=params,
        cost_estimate=pl.CostEstimate(
            flops=guess * BLK * unit * emb_width * 2,
            bytes_accessed=guess * BLK * unit * 2,
            transcendentals=guess * BLK * unit,
        ),
        name="table",
    )(ids, number, src_rows, dst_emb)

    vocab_slice = word_table.shape[0]
    local_ids = tokens.reshape(-1) - dst_place * vocab_slice
    onehot = (local_ids[:, None] == jnp.arange(vocab_slice, dtype=jnp.int32)[None, :]).astype(
        jnp.bfloat16
    )
    looked = jnp.dot(onehot, word_table, preferred_element_type=jnp.float32)
    word_rows = lax.psum(looked.astype(jnp.bfloat16), "dst")
    logits = lax.dot_general(
        word_rows, out_emb, (((1,), (1,)), ((), ())), preferred_element_type=jnp.float32
    )
    emission = jnp.exp(logits - log_norm[None, :]).reshape(STEPS, traces, col_count)
    emission_piece = lax.dynamic_slice_in_dim(emission, src_place * piece, piece, 2)

    allowed = jnp.repeat((mask == 1).T, unit, axis=1)
    row_best = jnp.max(jnp.where(allowed, top, very_negative), axis=0)
    row_mass = jnp.sum(jnp.where(allowed, mass * jnp.exp(top - row_best[None, :]), 0.0), axis=0)
    pairs = lax.all_gather(jnp.stack([row_best, row_mass]), "dst", axis=0)
    whole_best = jnp.max(pairs[:, 0], axis=0)
    whole_mass = jnp.sum(pairs[:, 1] * jnp.exp(pairs[:, 0] - whole_best[None]), axis=0)
    log_total = whole_best + jnp.log(whole_mass)
    factor = jnp.where(allowed, jnp.exp(top - log_total[None, :]), 0.0)

    def sweep(kind, alphas, weights):
        outs = [
            jax.ShapeDtypeStruct((traces, col_count), jnp.float32),
            jax.ShapeDtypeStruct((traces, row_count), jnp.float32),
        ]
        if kind:
            outs.append(jax.ShapeDtypeStruct((kind, traces, padded), jnp.float32))
        return pl.pallas_call(
            functools.partial(sweep_kernel, unit, cols, traces, kind),
            out_shape=tuple(outs),
            in_specs=[smem, smem] + [vmem] * (len(alphas) + 2) + [anywhere],
            out_specs=(vmem,) * len(outs),
            scratch_shapes=[
                pltpu.VMEM((DEPTH, BLK, unit), jnp.bfloat16),
                pltpu.SemaphoreType.DMA((DEPTH,)),
            ],
            compiler_params=params,
            cost_estimate=pl.CostEstimate(
                flops=guess * BLK * unit * traces * 4,
                bytes_accessed=guess * BLK * unit * 2,
                transcendentals=0,
            ),
            name="sweep%d" % kind,
        )(ids, number, *alphas, factor, weights, transit)

    def exchange(ahead, behind, position):
        def payload(value, scale, number):
            return jnp.concatenate(
                [
                    value.reshape(traces, number, piece).transpose(1, 0, 2),
                    jnp.broadcast_to(scale[None, :, None], (number, traces, LANES)),
                ],
                axis=2,
            )

        width = piece + LANES
        semaphores = pltpu.SemaphoreType.DMA((src_count + dst_count,))
        return pl.pallas_call(
            functools.partial(
                exchange_kernel, {"src": src_count, "dst": dst_count}, piece, states
            ),
            out_shape=(
                jax.ShapeDtypeStruct((traces, row_count), jnp.float32),
                jax.ShapeDtypeStruct((traces, col_count), jnp.float32),
            ),
            in_specs=[vmem] * 3,
            out_specs=(vmem, vmem),
            scratch_shapes=[
                pltpu.VMEM((src_count, traces, width), jnp.float32),
                pltpu.VMEM((dst_count, traces, width), jnp.float32),
                pltpu.VMEM((traces, width), jnp.float32),
                pltpu.VMEM((traces, width), jnp.float32),
                pltpu.VMEM((dst_count, traces, width), jnp.float32),
                pltpu.VMEM((src_count, traces, width), jnp.float32),
            ]
            + [semaphores] * 4,
            compiler_params=pltpu.CompilerParams(
                collective_id=0, has_side_effects=True, vmem_limit_bytes=VMEM_BYTES
            ),
            name="exchange",
        )(
            payload(ahead, jnp.sum(ahead * emission[position], axis=1), src_count),
            payload(behind, jnp.sum(behind, axis=1), dst_count),
            emission_piece[position],
        )

    last_weights = emission[2] * beta_end
    pred, carried = sweep(0, [alpha_rows], last_weights)
    alpha_1, beta_2 = exchange(pred, carried, 0)
    weights_2 = emission[1] * beta_2
    pred, carried, middle_terms = sweep(1, [alpha_1], weights_2)
    alpha_2, beta_1 = exchange(pred, carried, 1)
    weights_1 = emission[0] * beta_1
    pred, carried, end_terms = sweep(
        2, [alpha_2, alpha_rows], jnp.concatenate([weights_1, last_weights], axis=0)
    )

    block_terms = jnp.concatenate([middle_terms, end_terms], axis=0)[:, :, :places]
    scales = jnp.concatenate(
        [
            jnp.sum(pred * emission[2], axis=1)[None],
            jnp.sum(carried, axis=1)[None],
            jnp.sum(block_terms, axis=2),
        ],
        axis=0,
    )
    kinds = scales.shape[0]
    shape = (-(-kinds // 8) * 8, -(-traces // LANES) * LANES)
    totals = pl.pallas_call(
        functools.partial(total_kernel, {"src": src_count, "dst": dst_count}),
        out_shape=jax.ShapeDtypeStruct(shape, jnp.float32),
        in_specs=[vmem],
        out_specs=vmem,
        scratch_shapes=[
            pltpu.VMEM(shape, jnp.float32),
            pltpu.VMEM((src_count,) + shape, jnp.float32),
            pltpu.VMEM((dst_count,) + shape, jnp.float32),
        ]
        + [pltpu.SemaphoreType.DMA((src_count,))] * 2
        + [pltpu.SemaphoreType.DMA((dst_count,))] * 2,
        compiler_params=pltpu.CompilerParams(collective_id=1, has_side_effects=True),
        name="totals",
    )(jnp.pad(scales, ((0, shape[0] - kinds), (0, shape[1] - traces))))[:kinds, :traces]
    predicted = jnp.sum(lax.all_gather(pred, "src", axis=0), axis=0)
    alpha_end = predicted * emission[2] / (totals[0] / states)[:, None]

    parts = carried.reshape(traces, dst_count, piece).transpose(1, 0, 2)
    part = jnp.sum(lax.all_to_all(parts, "dst", 0, 0, tiled=False), axis=0)
    back = lax.ppermute(part, both, [(b, a) for a, b in moves])
    gathered = lax.all_gather(back, "dst", axis=1, tiled=True)
    beta_start = gathered / (totals[1] / states)[:, None]

    counts = jnp.sum(block_terms / totals[2:][:, :, None], axis=(0, 1)) * (
        NB * NB / (STEPS * traces)
    )
    counts = counts.reshape(units, cols)
    placed = jnp.sum(jnp.where(owner[:, :, None], counts[:, None, :], 0.0), axis=0)
    mask_rows = block_mask.shape[0]
    everyone = jnp.sum(lax.all_gather(placed, "src", axis=0), axis=0)
    block_counts = lax.dynamic_slice_in_dim(everyone, src_place * mask_rows, mask_rows, 0)
    return (alpha_end, beta_start, block_counts)


def solution(mesh):
    return jax.shard_map(
        local,
        mesh=mesh,
        in_specs=(
            P("src", None),
            P("dst", None),
            P("dst", None),
            P("dst", None),
            P("dst"),
            P("src", "dst"),
            P(),
            P(None, "src"),
            P(None, "dst"),
        ),
        out_specs=(P(None, "dst"), P(None, "src"), P("src", "dst")),
        check_vma=False,
    )
```

profile of v0, /device:TPU:1, one launch (start us, length us, event | category | flops | bytes accessed | tf_op | source)
XLA Modules:
  0.0 423.0 jit_solution(16880135280930544139)
XLA Ops:
  7.3 1.2 constant_dynamic-slice_fusion.1
  8.5 4.6 %collective-permute-start.1 = (bf16[2048,128]{1,0:T(8,128)(2,1)S(1)}, bf16[2048,128]{1,0:T(8,128)(2,1)S(1)}, u32[]{:S(2)}, u32[]{:S(2)}) collective-permute-start(bf16[2048,128]{1,0:T(8,128)(2,1)S(1)} %constant_dynamic-slice_fusion.1), channel_id=1, source_target_pairs={{0,0},{4,1},{8,2},{12,3},{16,4},{20,5},{24,6},{28,7},{1,8},{5,9},{... | collective-permute-start | bytes 1572872 | tf_op jit(solution)/shard_map/ppermute | solution.py:260
  13.1 6.8 %collective-permute-done.1 = bf16[2048,128]{1,0:T(8,128)(2,1)S(1)} collective-permute-done((bf16[2048,128]{1,0:T(8,128)(2,1)S(1)}, bf16[2048,128]{1,0:T(8,128)(2,1)S(1)}, u32[]{:S(2)}, u32[]{:S(2)}) %collective-permute-start.1) | collective-permute-done | bytes 524320 | tf_op jit(solution)/shard_map/ppermute | solution.py:260
  19.9 0.8 copy-done.6
  20.7 0.9 constant_dynamic-slice_fusion.2
  21.6 7.4 %collective-permute-start = (f32[8,2048]{1,0:T(8,128)S(1)}, f32[8,2048]{1,0:T(8,128)S(1)}, u32[]{:S(2)}, u32[]{:S(2)}) collective-permute-start(f32[8,2048]{1,0:T(8,128)S(1)} %constant_dynamic-slice_fusion.2), channel_id=1, source_target_pairs={{0,0},{4,1},{8,2},{12,3},{16,4},{20,5},{24,6},{28,7},{1,8},{5,9},{... | collective-permute-start | bytes 196616 | tf_op jit(solution)/shard_map/ppermute | solution.py:266
  29.0 24.2 %all-gather.3 = s32[4,32,16]{1,2,0:T(8,128)S(1)} all-gather(s32[1,32,16]{1,2,0:T(8,128)} %bitcast.69), channel_id=1, replica_groups=mesh['src'=4,'dst'=8] {'src'}, dimensions={0}, use_global_device_ids=true | all-gather | bytes 10240 | tf_op jit(solution)/shard_map/all_gather | solution.py:269
  55.4 1.5 convolution_convert_fusion
  56.9 16.4 %psum.7 = bf16[24,128]{1,0:T(8,128)(2,1)S(1)} all-reduce(bf16[24,128]{1,0:T(8,128)(2,1)S(1)} %convolution_convert_fusion), channel_id=1, replica_groups=mesh['src'=4,'dst'=8] {'dst'}, use_global_device_ids=true, to_apply=%region_8.9 | all-reduce | flops 3072 | bytes 12288 | tf_op jit(solution)/shard_map/psum | solution.py:321
  73.5 0.9 select_reduce_fusion.2.ids
  74.3 1.2 fusion
  75.6 1.2 all-gather.9.cloned.1.call-done.src
  76.7 59.9 %table.1 = (f32[16,16384]{1,0:T(8,128)}, f32[16,16384]{1,0:T(8,128)}, bf16[512,512,512]{2,1,0:T(8,128)(2,1)}) custom-call(s32[512]{0:T(512)} %select_reduce_fusion.2.ids, s32[1]{0:T(128)} %bitcast.1.count, bf16[16384,128]{1,0:T(8,128)(2,1)} %all-gather.9.cloned.1.call-done.src, bf16[8192,128]{1,0:T(8,128)(2,1)} %dst.1), custom_call_target="tpu_custom_call" | custom-call | flops 6912212992 | bytes 54001664 | tf_op jit(solution)/shard_map/table/pallas_call | solution.py:293
  136.7 1.6 select_reduce_fusion.1
  138.3 1.6 select_reduce_fusion
  139.9 0.8 maximum_bitcast_fusion
  140.8 0.7 slice_multiply_fusion.2.refs_2_
  142.1 18.9 %all_gather.31.refs_0_.refs_1_ = f32[8,16384]{1,0:T(8,128)} all-gather(f32[8,2048]{1,0:T(8,128)S(1)} %collective-permute-done), channel_id=1, replica_groups=mesh['src'=4,'dst'=8] {'dst'}, dimensions={1}, use_global_device_ids=true | all-gather | bytes 589824 | tf_op jit(solution)/shard_map/all_gather | solution.py:267
  161.1 15.3 %all-gather.13.cloned.1.call-done = f32[8,2,16384]{2,1,0:T(2,128)} async-done(((f32[1,2,16384]{2,1,0:T(2,128)}), f32[8,2,16384]{2,1,0:T(2,128)}) %all-gather.13.cloned.1.call-update) | async-done | bytes 1048592 | tf_op jit(solution)/shard_map/all_gather | solution.py:331
  176.4 2.9 fusion.11
  179.3 0.8 fusion.4
  180.1 1.2 exponential_select_fusion.refs_1_.refs_2_
  181.3 31.4 %sweep0.1 = (f32[8,8192]{1,0:T(8,128)}, f32[8,16384]{1,0:T(8,128)}) custom-call(s32[512]{0:T(512)} %select_reduce_fusion.2.ids, s32[1]{0:T(128)} %bitcast.1.count, f32[8,16384]{1,0:T(8,128)} %all_gather.31.refs_0_.refs_1_, f32[16,16384]{1,0:T(8,128)} %exponential_select_fusion.refs_1_.refs_2_, f32[8,8192]{1,0:T(8,128)} %slice_multiply_fusion.2.refs_2_, ...), custom_call_target="tpu_custom_call" | custom-call | flops 864026624 | bytes 54001664 | tf_op jit(solution)/shard_map/sweep0/pallas_call | solution.py:344
  212.7 1.2 multiply_reduce_fusion.2
  213.9 1.3 reduce_sum.169
  215.3 1.9 pad_maximum_fusion.behind
  218.0 24.9 %exchange.2 = (f32[8,16384]{1,0:T(8,128)}, f32[8,8192]{1,0:T(8,128)}) custom-call(f32[4,8,2176]{2,1,0:T(8,128)} %pad_maximum_fusion.3.ahead, f32[8,8,2176]{2,1,0:T(8,128)} %pad_maximum_fusion.behind, f32[8,2048]{1,0:T(8,128)} %get-tuple-element.39.glow), custom_call_target="tpu_custom_call" | custom-call | tf_op jit(solution)/shard_map/exchange/pallas_call | solution.py:374
  242.9 1.7 slice_multiply_fusion.refs_2_
  244.6 38.0 %sweep1.1 = (f32[8,8192]{1,0:T(8,128)}, f32[8,16384]{1,0:T(8,128)}, f32[1,8,512]{2,1,0:T(8,128)}) custom-call(s32[512]{0:T(512)} %select_reduce_fusion.2.ids, s32[1]{0:T(128)} %bitcast.1.count, f32[8,16384]{1,0:T(8,128)} %get-tuple-element.23.refs_0_, f32[16,16384]{1,0:T(8,128)} %exponential_select_fusion.refs_1_.refs_2_, ...), custom_call_target="tpu_custom_call" | custom-call | flops 864026624 | bytes 54001664 | tf_op jit(solution)/shard_map/sweep1/pallas_call | solution.py:344
  282.6 1.3 reduce_sum.171
  283.9 1.2 multiply_reduce_fusion.1
  285.2 1.9 pad_maximum_fusion.1.behind
  287.9 25.9 %exchange.3 = (f32[8,16384]{1,0:T(8,128)}, f32[8,8192]{1,0:T(8,128)}) custom-call(f32[4,8,2176]{2,1,0:T(8,128)} %pad_maximum_fusion.4.ahead, f32[8,8,2176]{2,1,0:T(8,128)} %pad_maximum_fusion.1.behind, f32[8,2048]{1,0:T(8,128)} %get-tuple-element.38.glow), custom_call_target="tpu_custom_call" | custom-call | tf_op jit(solution)/shard_map/exchange/pallas_call | solution.py:374
  313.7 1.0 slice_multiply_fusion.1
  314.7 0.8 pad_maximum_fusion.2.refs_3_
  315.6 38.4 %sweep2.1 = (f32[8,8192]{1,0:T(8,128)}, f32[8,16384]{1,0:T(8,128)}, f32[2,8,512]{2,1,0:T(8,128)}) custom-call(s32[512]{0:T(512)} %select_reduce_fusion.2.ids, s32[1]{0:T(128)} %bitcast.1.count, f32[8,16384]{1,0:T(8,128)} %get-tuple-element.27.refs_0_, f32[8,16384]{1,0:T(8,128)} %all_gather.31.refs_0_.refs_1_, ...), custom_call_target="tpu_custom_call" | custom-call | flops 864026624 | bytes 54001664 | tf_op jit(solution)/shard_map/sweep2/pallas_call | solution.py:344
  354.0 1.1 multiply_reduce_fusion
  355.2 0.8 constant_dynamic-update-slice_fusion
  356.1 1.3 reduce_sum.174
  358.0 18.2 %totals.1 = f32[8,128]{1,0:T(8,128)} custom-call(f32[8,128]{1,0:T(8,128)} %select_maximum_fusion.value), custom_call_target="tpu_custom_call" | custom-call | tf_op jit(solution)/shard_map/totals/pallas_call | solution.py:425
  377.0 3.6 all-to-all-start
  380.9 10.4 %all-gather.2 = f32[512,16]{0,1:T(8,128)S(1)} all-gather(f32[128,16]{0,1:T(8,128)S(1)} %select_reduce_fusion.4), channel_id=4, replica_groups=mesh['src'=4,'dst'=8] {'src'}, dimensions={0}, use_global_device_ids=true | all-gather | bytes 40960 | tf_op jit(solution)/shard_map/all_gather | solution.py:455
  391.3 0.8 multiply_bitcast_fusion
  392.1 6.3 %collective-permute-start.2 = (f32[8,2048]{1,0:T(8,128)S(1)}, f32[8,2048]{1,0:T(8,128)S(1)}, u32[]{:S(2)}, u32[]{:S(2)}) collective-permute-start(f32[8,2048]{1,0:T(8,128)S(1)} %reduce_sum.176), channel_id=1, source_target_pairs={{0,0},{1,4},{2,8},{3,12},{4,16},{5,20},{6,24},{7,28},{8,1},{9,5},{... | collective-permute-start | bytes 196616 | tf_op jit(solution)/shard_map/ppermute | solution.py:445
  399.7 13.7 %all_gather.37 = f32[8,16384]{1,0:T(8,128)S(1)} all-gather(f32[8,2048]{1,0:T(8,128)S(1)} %collective-permute-done.2), channel_id=1, replica_groups=mesh['src'=4,'dst'=8] {'dst'}, dimensions={1}, use_global_device_ids=true | all-gather | bytes 589824 | tf_op jit(solution)/shard_map/all_gather | solution.py:446
  413.4 0.9 broadcast_divide_fusion
  414.4 1.3 bitcast_reduce_fusion
  415.7 0.8 multiply_divide_fusion
  (68 shorter events, 8.0 us)
Async XLA Ops:
  7.2 67.2 %copy-start = (bf16[8192,128]{1,0:T(8,128)(2,1)S(1)}, bf16[8192,128]{1,0:T(8,128)(2,1)}, u32[]{:S(2)}) copy-start(bf16[8192,128]{1,0:T(8,128)(2,1)} %param.11) | copy-start | bytes 6291460
  7.2 48.1 %copy-start.12 = (s32[3,8]{1,0:T(4,128)S(1)}, s32[3,8]{1,0:T(4,128)}, u32[]{:S(2)}) copy-start(s32[3,8]{1,0:T(4,128)} %param.15) | copy-start | bytes 292
  7.2 67.1 %copy-start.10 = (f32[8192]{0:T(1024)S(1)}, f32[8192]{0:T(1024)}, u32[]{:S(2)}) copy-start(f32[8192]{0:T(1024)} %param.13) | copy-start | bytes 98308
  7.2 69.5 %all-gather.9.cloned.1.call-start = ((), (), s32[]{:S(2)}) async-start(), calls=%async_computation.1 | async-start | bytes 4718592 | tf_op jit(solution)/shard_map/all_gather | solution.py:261
  8.5 11.4 %collective-permute-start.1 = (bf16[2048,128]{1,0:T(8,128)(2,1)S(1)}, bf16[2048,128]{1,0:T(8,128)(2,1)S(1)}, u32[]{:S(2)}, u32[]{:S(2)}) collective-permute-start(bf16[2048,128]{1,0:T(8,128)(2,1)S(1)} %constant_dynamic-slice_fusion.1), channel_id=1, source_target_pairs={{0,0},{4,1},{8,2},{12,3},{16,4},{20,5},{24,6},{28,7},{1,8},{5,9},{... | collective-permute-start | bytes 1572872 | tf_op jit(solution)/shard_map/ppermute | solution.py:260
  19.9 0.8 copy-start.6
  20.7 155.7 %all-gather.13.cloned.1.call-start = ((), (), s32[]{:S(2)}) async-start(), calls=%async_computation.3 | async-start | bytes 1179648 | tf_op jit(solution)/shard_map/all_gather | solution.py:331
  21.6 120.6 %collective-permute-start = (f32[8,2048]{1,0:T(8,128)S(1)}, f32[8,2048]{1,0:T(8,128)S(1)}, u32[]{:S(2)}, u32[]{:S(2)}) collective-permute-start(f32[8,2048]{1,0:T(8,128)S(1)} %constant_dynamic-slice_fusion.2), channel_id=1, source_target_pairs={{0,0},{4,1},{8,2},{12,3},{16,4},{20,5},{24,6},{28,7},{1,8},{5,9},{... | collective-permute-start | bytes 196616 | tf_op jit(solution)/shard_map/ppermute | solution.py:266
  53.4 1.4 copy-start.8
  136.6 1.6 copy-start.1
  136.7 4.1 copy-start.7
  140.7 273.7 %all-gather.11.cloned.1.call-start = ((), (), s32[]{:S(2)}) async-start(), calls=%async_computation.2 | async-start | bytes 1310720 | tf_op jit(solution)/shard_map/all_gather | solution.py:440
  176.4 3.7 copy-start.2
  212.7 4.5 %copy-start.5 = (f32[8,8192]{1,0:T(8,128)S(1)}, f32[8,8192]{1,0:T(8,128)}, u32[]{:S(2)}) copy-start(f32[8,8192]{1,0:T(8,128)} %get-tuple-element.21) | copy-start | bytes 786436
  282.6 4.6 %copy-start.4 = (f32[8,8192]{1,0:T(8,128)S(1)}, f32[8,8192]{1,0:T(8,128)}, u32[]{:S(2)}) copy-start(f32[8,8192]{1,0:T(8,128)} %get-tuple-element.25) | copy-start | bytes 786436
  283.9 30.8 %copy-start.3 = (f32[8,8192]{1,0:T(8,128)S(1)}, f32[8,8192]{1,0:T(8,128)}, u32[]{:S(2)}) copy-start(f32[8,8192]{1,0:T(8,128)} %slice_multiply_fusion.2.refs_2_) | copy-start | bytes 786436
  315.6 39.6 %copy-start.11 = (f32[1,8,512]{2,1,0:T(8,128)S(1)}, f32[1,8,512]{2,1,0:T(8,128)}, u32[]{:S(2)}) copy-start(f32[1,8,512]{2,1,0:T(8,128)} %get-tuple-element.31) | copy-start | bytes 49156
  354.0 26.7 %copy-start.9 = (pred[32,128]{1,0:T(8,128)(4,1)S(1)}, pred[32,128]{1,0:T(8,128)(4,1)}, u32[]{:S(2)}) copy-start(pred[32,128]{1,0:T(8,128)(4,1)} %copy-done.8) | copy-start | bytes 12292
  377.0 15.1 %all-to-all-start = ((f32[8,8,2048]{2,1,0:T(8,128)}), f32[8,8,2048]{2,1,0:T(8,128)S(1)}, u32[]{:S(2)}, u32[]{:S(2)}) async-start(f32[8,8,2048]{2,1,0:T(8,128)} %bitcast.60), calls=%async_computation | async-start | bytes 1048576 | tf_op jit(solution)/shard_map/all_to_all | solution.py:444
  392.1 7.6 %collective-permute-start.2 = (f32[8,2048]{1,0:T(8,128)S(1)}, f32[8,2048]{1,0:T(8,128)S(1)}, u32[]{:S(2)}, u32[]{:S(2)}) collective-permute-start(f32[8,2048]{1,0:T(8,128)S(1)} %reduce_sum.176), channel_id=1, source_target_pairs={{0,0},{1,4},{2,8},{3,12},{4,16},{5,20},{6,24},{7,28},{8,1},{9,5},{... | collective-permute-start | bytes 196616 | tf_op jit(solution)/shard_map/ppermute | solution.py:445
Sparse Core Ops, SparseCore 0:
  20.8 55.8 all-gather.8
  140.8 35.5 all-gather.12
  355.3 34.8 all-gather.10
where the time goes:
time: 429 us; the launch traced here: 423 us
  Pallas kernels  237 us (55%)
  blocking collectives  83.6 us (19%)
  other arithmetic  33 us (8%)
  waiting for transfers between devices  24 us (6%)
  starting transfers between devices  22 us (5%)
  between operations  14.1 us (3%)
  local copies, waits for them, and re-layouts  6.81 us (2%)
    pallas_call x3, Pallas kernels, sweep(): pl.pallas_call(functools.partial(sweep_kernel, unit, cols, traces, kind),...  108 us
    pallas_call x1, Pallas kernels, local(): pl.pallas_call(functools.partial(table_kernel, unit, cols), out_shape=(ja...  59.9 us
    pallas_call x2, Pallas kernels, exchange(): pl.pallas_call(functools.partial(exchange_kernel, {'src': src_count, 'dst...  50.8 us
    all_gather x1, blocking collectives, local(): whole_mask = lax.all_gather(block_mask, 'src', axis=0, tiled=True)  24.2 us
    all_gather x1, blocking collectives, local(): alpha_rows = lax.all_gather(alpha_moved, 'dst', axis=1, tiled=True)  18.9 us
    pallas_call x1, Pallas kernels, local(): pl.pallas_call(functools.partial(total_kernel, {'src': src_count, 'dst':...  18.2 us
    psum x1, blocking collectives, local(): word_rows = lax.psum(looked.astype(jnp.bfloat16), 'dst')  16.4 us
    all_gather x1, waiting for transfers between devices, local(): pairs = lax.all_gather(jnp.stack([row_best, row_mass]), 'dst', axis=0)  15.3 us
  transfers between devices with their start and end apart: 7, of which 4 were waited for; matrix products, arithmetic and copies ran while one was open for 4% of the time, Pallas kernels for 18%

commit v1 on v0

v1 whole, which is shorter than its diff:
```python
import functools

import jax
import jax.numpy as jnp
from jax import lax
from jax.experimental import pallas as pl
from jax.experimental.pallas import tpu as pltpu
from jax.sharding import PartitionSpec as P

BLK = 512
STEPS = 3
LANES = 128
DEPTH = 8
very_negative = -1e30
GROUP = 4
HELD_BYTES = 40 * 1024 * 1024
TABLE_BYTES = 16 * 1024 * 1024
VMEM_BYTES = 16 * 1024 * 1024


def table_kernel(
    unit, cols, held, ids, count, src, dst, top, mass, near, far,
    buf_0, buf_1, scores_0, scores_1, best_0, best_1, sems,
):
    number = count[0]
    chunk = min(128, unit)
    pieces = unit // chunk
    top[...] = jnp.full_like(top, very_negative)
    mass[...] = jnp.zeros_like(mass)

    def place(slot):
        entry = ids[slot]
        return lax.div(entry, cols), lax.rem(entry, cols)

    def score(slot, scores, best, c):
        i, j = place(slot)
        d = dst[pl.ds(pl.multiple_of(j * BLK, BLK), BLK), :]
        value = lax.dot_general(
            d, src[pl.ds(pl.multiple_of(i * unit + c * chunk, chunk), chunk), :],
            (((1,), (1,)), ((), ())), preferred_element_type=jnp.float32,
        )
        scores[:, c * chunk:(c + 1) * chunk] = value
        best[:, c * chunk:(c + 1) * chunk] = jnp.max(value, axis=0, keepdims=True)

    def phase(slot, scores, best, later, scores_next, best_next, put):
        sums = []
        for c in range(pieces):
            score(later, scores_next, best_next, c)
            span = slice(c * chunk, (c + 1) * chunk)
            risen = jnp.exp(scores[:, span] - best[:, span])
            put(span, risen.astype(jnp.bfloat16))
            sums.append(jnp.sum(risen, axis=0, keepdims=True))
        i, j = place(slot)
        rows = pl.ds(pl.multiple_of(i * unit, unit), unit)
        top[pl.ds(j, 1), rows] = best[...]
        mass[pl.ds(j, 1), rows] = jnp.concatenate(sums, axis=1)

    def run(low, high, out):
        for c in range(pieces):
            score(low, scores_0, best_0, c)

        def body(p, carry):
            even = low + 2 * p
            odd = jnp.minimum(even + 1, high - 1)
            after = jnp.minimum(even + 2, high - 1)
            with_even, with_odd = out(p, even, odd, high)
            with_even(lambda put: phase(even, scores_0, best_0, odd, scores_1, best_1, put))
            with_odd(lambda put: phase(odd, scores_1, best_1, after, scores_0, best_0, put))
            return carry

        lax.fori_loop(0, lax.div(high - low + 1, 2), body, 0)

    def keep(p, even, odd, high):
        def store(slot):
            def put(span, value):
                near[slot, :, span] = value

            return put

        return lambda go: go(store(even)), lambda go: go(store(odd))

    def copy(slot, buf, b):
        return pltpu.make_async_copy(buf, far.at[slot - held], sems.at[b])

    def send(p, even, odd, high):
        def through(slot, buf, b, live):
            def put(span, value):
                buf[:, span] = value

            def go(step):
                @pl.when(p > 0)
                def _():
                    copy(slot, buf, b).wait()

                step(put)

                @pl.when(live)
                def _():
                    copy(slot, buf, b).start()

            return go

        return through(even, buf_0, 0, even < high), through(odd, buf_1, 1, even + 1 < high)

    @pl.when(number > held)
    def _():
        run(held, number, send)

    @pl.when(number > 0)
    def _():
        run(0, jnp.minimum(number, held), keep)

    @pl.when(number > held)
    def _():
        copy(held, buf_0, 0).wait()

    @pl.when((number > held) & (lax.rem(number - held, 2) == 0))
    def _():
        copy(held, buf_1, 1).wait()


def sweep_kernel(unit, cols, held, traces, kind, ids, count, *refs):
    if kind == 2:
        alpha, early, factor, weight, last, near, far, pred, carried, terms, buf, sems = refs
    elif kind == 1:
        alpha, factor, weight, near, far, pred, carried, terms, buf, sems = refs
    else:
        alpha, factor, weight, near, far, pred, carried, buf, sems = refs
    number = count[0]
    pred[...] = jnp.zeros_like(pred)
    carried[...] = jnp.zeros_like(carried)
    if kind:
        terms[...] = jnp.zeros_like(terms)

    def copy(slot):
        b = lax.rem(slot - held, DEPTH)
        return pltpu.make_async_copy(far.at[slot - held], buf.at[b], sems.at[b])

    for p in range(DEPTH):

        @pl.when(held + p < number)
        def _():
            copy(held + p).start()

    def group(slots, high, tile):
        found = []
        for slot in slots:
            real = jnp.minimum(slot, high - 1)
            entry = ids[real]
            i = lax.div(entry, cols)
            j = lax.rem(entry, cols)
            rows = pl.ds(pl.multiple_of(i * unit, unit), unit)
            places = pl.ds(pl.multiple_of(j * BLK, BLK), BLK)
            share = factor[pl.ds(j, 1), rows] * jnp.where(slot < high, 1.0, 0.0)
            mix = (alpha[:, rows] * share).astype(jnp.bfloat16)
            block = tile(real)
            ahead = lax.dot_general(
                mix, block, (((1,), (1,)), ((), ())), preferred_element_type=jnp.float32
            )
            spread = jnp.dot(weight[:, places], block, preferred_element_type=jnp.float32)
            values = []
            if kind == 1:
                values.append(mix.astype(jnp.float32) * spread)
            elif kind == 2:
                first = (early[:, rows] * share).astype(jnp.bfloat16)
                values.append(first.astype(jnp.float32) * spread)
                values.append(last[:, places].astype(jnp.float32) * ahead)
            values = [jnp.sum(v, axis=1, keepdims=True) for v in values]
            found.append((i, j, rows, places, ahead, share * spread, values))
        for i, j, rows, places, ahead, behind, values in found:
            pred[:, places] += ahead
            carried[:, rows] += behind
            for t, value in enumerate(values):
                hit = lax.broadcasted_iota(jnp.int32, terms.shape[2:], 1) == j
                terms[t, i] += jnp.where(hit, value, 0.0)

    near_count = jnp.minimum(number, held)

    def near_body(g, carry):
        group([g * GROUP + u for u in range(GROUP)], near_count, lambda slot: near[slot])
        return carry

    lax.fori_loop(0, lax.div(near_count + GROUP - 1, GROUP), near_body, 0)

    def far_body(g, carry):
        slots = [held + g * GROUP + u for u in range(GROUP)]
        for slot in slots:

            @pl.when(slot < number)
            def _():
                copy(slot).wait()

        group(slots, number, lambda slot: buf[lax.rem(slot - held, DEPTH)])
        for slot in slots:

            @pl.when(slot + DEPTH < number)
            def _():
                copy(slot + DEPTH).start()

        return carry

    far_count = number - near_count
    lax.fori_loop(0, lax.div(far_count + GROUP - 1, GROUP), far_body, 0)


class Lines:
    def __init__(self, lines):
        self.lines = lines
        self.place = {name: lax.axis_index(name) for name in lines}

    def peer(self, name, k):
        return lax.rem(self.place[name] + k, self.lines[name])

    def origin(self, name, k):
        return lax.rem(self.place[name] + self.lines[name] - k, self.lines[name])

    def greet(self):
        barrier = pltpu.get_barrier_semaphore()
        for name in self.lines:
            for k in range(1, self.lines[name]):
                pl.semaphore_signal(
                    barrier, inc=1, device_id={name: self.peer(name, k)},
                    device_id_type=pl.DeviceIdType.MESH,
                )

    def gather_in(self, more=0):
        total = sum(self.lines.values()) - len(self.lines) + more
        pl.semaphore_wait(pltpu.get_barrier_semaphore(), total)

    def send(self, name, source, landing, send, recv):
        copies = []
        for k in range(1, self.lines[name]):
            copy = pltpu.make_async_remote_copy(
                src_ref=source(self.peer(name, k)),
                dst_ref=landing.at[k],
                send_sem=send.at[k],
                recv_sem=recv.at[k],
                device_id={name: self.peer(name, k)},
                device_id_type=pl.DeviceIdType.MESH,
            )
            copy.start()
            copies.append(copy)
        return copies


def stats_kernel(
    lines, piece, top, mass, alpha, near, factor, spread_alpha,
    parts, land, merged, land_2, land_a, *sems,
):
    net = Lines(lines)
    net.greet()
    count = lines["dst"]
    for p in range(count):
        rows = slice(p * piece, (p + 1) * piece)
        best = jnp.max(top[:, rows], axis=0, keepdims=True)
        total = jnp.sum(mass[:, rows] * jnp.exp(top[:, rows] - best), axis=0, keepdims=True)
        parts[p] = jnp.where(
            total > 0.0, best + jnp.log(jnp.maximum(total, 1e-37)), very_negative
        )
    net.gather_in()
    first = net.send("dst", lambda peer: parts.at[peer], land, sems[0], sems[1])
    sent = net.send("dst", lambda peer: alpha, land_a, sems[4], sems[5])
    land[0] = parts[net.place["dst"]]
    for copy in first:
        copy.wait_recv()
    best = land[0]
    for k in range(1, count):
        best = jnp.maximum(best, land[k])
    total = jnp.zeros_like(best)
    for k in range(count):
        total = total + jnp.exp(land[k] - best)
    merged[...] = best + jnp.log(total)
    second = net.send("dst", lambda peer: merged, land_2, sems[2], sems[3])

    def finish(k, level):
        rows = pl.ds(pl.multiple_of(net.origin("dst", k) * piece, piece), piece)
        factor[:, rows] = jnp.exp(top[:, rows] - level)

    finish(0, merged[...])
    for k in range(count):
        rows = pl.ds(pl.multiple_of(net.origin("dst", k) * piece, piece), piece)
        if k:
            sent[k - 1].wait_recv()
        spread_alpha[:, rows] = (alpha[...] if k == 0 else land_a[k]).astype(jnp.float32)
    for k in range(1, count):
        second[k - 1].wait_recv()
        finish(k, land_2[k])
    for copy in first + second + sent:
        copy.wait_send()


def exchange_kernel(
    lines, piece, states, pred, carried, glow, glow_next, near, alpha, weights,
    out_f, out_b, in_f, in_b, red_f, red_b, land_f, land_b, *sems,
):
    net = Lines(lines)
    net.greet()
    shape = (pred.shape[0], LANES)
    total_f = jnp.broadcast_to(
        jnp.sum(pred[...] * glow[...], axis=1, keepdims=True), shape
    ).astype(jnp.bfloat16)
    total_b = jnp.broadcast_to(
        jnp.sum(carried[...], axis=1, keepdims=True), shape
    ).astype(jnp.bfloat16)
    payload = {"src": (out_f, pred, total_f), "dst": (out_b, carried, total_b)}
    for name, (out, value, total) in payload.items():
        for p in range(lines[name]):
            out[p, :, :piece] = value[:, p * piece:(p + 1) * piece].astype(jnp.bfloat16)
            out[p, :, piece:] = total
    net.gather_in()
    landing = {"src": in_f, "dst": in_b}
    first = {}
    for n, name in enumerate(("src", "dst")):
        out = payload[name][0]
        first[name] = net.send(
            name, lambda peer, out=out: out.at[peer], landing[name], sems[n], sems[2 + n]
        )
    second = {}
    order = (("src", "dst", red_f, land_f), ("dst", "src", red_b, land_b))
    for n, (name, other, red, land) in enumerate(order):
        value = payload[name][0][net.place[name]].astype(jnp.float32)
        for k in range(1, lines[name]):
            first[name][k - 1].wait_recv()
            value = value + landing[name][k].astype(jnp.float32)
        part, total = value[:, :piece], value[:, piece:]
        if name == "src":
            start = pl.multiple_of(net.place["src"] * piece, piece)
            part = part * glow[:, pl.ds(start, piece)]
        red[:, :piece] = part.astype(jnp.bfloat16)
        red[:, piece:] = total.astype(jnp.bfloat16)
        second[other] = net.send(
            other, lambda peer, red=red: red, land, sems[4 + n], sems[6 + n]
        )
    for name, red, land in (("dst", red_f, land_f), ("src", red_b, land_b)):
        total = red[:, piece:piece + 1].astype(jnp.float32)
        for k in range(1, lines[name]):
            second[name][k - 1].wait_recv()
            total = total + land[k, :, piece:piece + 1].astype(jnp.float32)
        scale = states / total
        for k in range(lines[name]):
            part = red[:, :piece] if k == 0 else land[k, :, :piece]
            start = pl.multiple_of(net.origin(name, k) * piece, piece)
            part = part.astype(jnp.float32) * scale
            if name == "dst":
                alpha[:, pl.ds(start, piece)] = part
            else:
                part = part * glow_next[:, pl.ds(start, piece)]
                weights[:, pl.ds(start, piece)] = part.astype(jnp.bfloat16)
    for copies in (*first.values(), *second.values()):
        for copy in copies:
            copy.wait_send()


def final_kernel(
    lines, piece, states, norm, pred, carried, glow, mid_terms, end_terms, owner,
    alpha, beta, counts,
    out_f, in_f, red_f, land_f, out_b, in_b, red_b, natural, land_b,
    sums, in_s, red_s, land_s, mine, in_c, *sems,
):
    net = Lines(lines)
    net.greet()
    src, dst = lines["src"], lines["dst"]
    traces = pred.shape[0]
    shape = (traces, LANES)
    number = net.place["dst"] * src + net.place["src"]
    to_src, to_dst = lax.div(number, dst), lax.rem(number, dst)
    held = net.place["src"] * dst + net.place["dst"]
    from_dst, from_src = lax.div(held, src), lax.rem(held, src)
    away = (to_src != net.place["src"]) | (to_dst != net.place["dst"])
    barrier = pltpu.get_barrier_semaphore()

    @pl.when(away)
    def _():
        for s, d in ((to_src, to_dst), (from_src, from_dst)):
            pl.semaphore_signal(
                barrier, inc=1, device_id={"src": s, "dst": d},
                device_id_type=pl.DeviceIdType.MESH,
            )

    terms = [mid_terms[0], end_terms[0], end_terms[1]]
    rows = [jnp.sum(pred[...] * glow[...], axis=1, keepdims=True)]
    rows.append(jnp.sum(carried[...], axis=1, keepdims=True))
    for t in terms:
        rows.append(jnp.sum(jnp.sum(t, axis=0), axis=1, keepdims=True))
    for n, row in enumerate(rows):
        sums[n] = jnp.broadcast_to(row, shape)
    for p in range(src):
        out_f[p] = pred[:, p * piece:(p + 1) * piece]
    for p in range(dst):
        out_b[p] = carried[:, p * piece:(p + 1) * piece]

    @pl.when(away)
    def _():
        net.gather_in(2)

    @pl.when(jnp.logical_not(away))
    def _():
        net.gather_in()

    first_s = net.send("src", lambda peer: sums, in_s, sems[0], sems[1])
    first_b = net.send("dst", lambda peer: out_b.at[peer], in_b, sems[2], sems[3])
    first_f = net.send("src", lambda peer: out_f.at[peer], in_f, sems[4], sems[5])

    total = sums[...]
    for k in range(1, src):
        first_s[k - 1].wait_recv()
        total = total + in_s[k]
    red_s[...] = total
    second_s = net.send("dst", lambda peer: red_s, land_s, sems[6], sems[7])

    value = out_f[net.place["src"]]
    for k in range(1, src):
        first_f[k - 1].wait_recv()
        value = value + in_f[k]
    start = pl.multiple_of(net.place["src"] * piece, piece)
    red_f[...] = value * glow[:, pl.ds(start, piece)]
    second_f = net.send("src", lambda peer: red_f, land_f, sems[8], sems[9])

    value = out_b[net.place["dst"]]
    for k in range(1, dst):
        first_b[k - 1].wait_recv()
        value = value + in_b[k]
    red_b[...] = value
    move = pltpu.make_async_remote_copy(
        src_ref=red_b, dst_ref=natural, send_sem=sems[10].at[0], recv_sem=sems[10].at[1],
        device_id={"src": to_src, "dst": to_dst}, device_id_type=pl.DeviceIdType.MESH,
    )

    @pl.when(away)
    def _():
        move.start()

    total = red_s[...]
    for k in range(1, dst):
        second_s[k - 1].wait_recv()
        total = total + land_s[k]
    level = jnp.zeros(mine.shape, jnp.float32)
    for t in range(len(terms)):
        share = norm / total[2 + t]
        level = level + jnp.sum(terms[t] * share[None], axis=1)
    mine[...] = level
    third_c = net.send("src", lambda peer: mine, in_c, sems[11], sems[12])

    @pl.when(away)
    def _():
        move.wait_recv()

    @pl.when(jnp.logical_not(away))
    def _():
        natural[...] = red_b[...]

    third_b = net.send("dst", lambda peer: natural, land_b, sems[13], sems[14])

    scale = states / total[0][:, :1]
    for k in range(src):
        if k:
            second_f[k - 1].wait_recv()
        part = red_f[...] if k == 0 else land_f[k]
        begin = pl.multiple_of(net.origin("src", k) * piece, piece)
        alpha[:, pl.ds(begin, piece)] = part * scale
    value = jnp.zeros(counts.shape, jnp.float32)
    for k in range(src):
        if k:
            third_c[k - 1].wait_recv()
        value = value + jnp.dot(
            owner[net.origin("src", k)], mine[...] if k == 0 else in_c[k],
            precision=lax.Precision.HIGHEST, preferred_element_type=jnp.float32,
        )
    counts[...] = value
    scale = states / total[1][:, :1]
    for k in range(dst):
        if k:
            third_b[k - 1].wait_recv()
        part = natural[...] if k == 0 else land_b[k]
        begin = pl.multiple_of(net.origin("dst", k) * piece, piece)
        beta[:, pl.ds(begin, piece)] = part * scale

    @pl.when(away)
    def _():
        move.wait_send()

    for copies in (first_s, first_b, first_f, second_s, second_f, third_c, third_b):
        for copy in copies:
            copy.wait_send()


def local(
    src_emb, dst_emb, out_emb, word_table, log_norm, block_mask, tokens, alpha_start, beta_end
):
    row_count, emb_width = src_emb.shape
    col_count = dst_emb.shape[0]
    traces = alpha_start.shape[0]
    src_count = lax.axis_size("src")
    dst_count = lax.axis_size("dst")
    states = row_count * src_count
    group = dst_count // src_count
    piece = col_count // src_count
    unit = min(BLK, piece)
    units = row_count // unit
    cols = col_count // BLK
    places = units * cols
    padded = -(-places // LANES) * LANES
    src_place = lax.axis_index("src")
    dst_place = lax.axis_index("dst")
    both = ("src", "dst")
    moves = [
        ((d // group) * dst_count + (d % group) * src_count + z, z * dst_count + d)
        for z in range(src_count)
        for d in range(dst_count)
    ]

    def spread_rows(mine):
        moved = lax.ppermute(mine, both, moves)
        return lax.all_gather(moved, "dst", axis=0, tiled=True)

    mine = lax.dynamic_slice_in_dim(src_emb, dst_place * piece, piece, 0)
    src_rows = spread_rows(mine)
    alpha_piece = lax.dynamic_slice_in_dim(alpha_start, dst_place * piece, piece, 1)
    alpha_moved = lax.ppermute(alpha_piece, both, moves)

    whole_mask = lax.all_gather(block_mask, "src", axis=0, tiled=True)
    unit_index = jnp.arange(units, dtype=jnp.int32)
    per_piece = piece // unit
    unit_state = (
        (unit_index // per_piece) * col_count + src_place * piece + (unit_index % per_piece) * unit
    )
    unit_block = unit_state // BLK
    owner = unit_block[:, None] == jnp.arange(whole_mask.shape[0], dtype=jnp.int32)[None, :]
    mask = jnp.sum(jnp.where(owner[:, :, None], whole_mask[None], 0), axis=1)
    flat = (mask == 1).reshape(places)
    index = jnp.arange(places, dtype=jnp.int32)
    before = jnp.sum(
        jnp.where((index[None, :] < index[:, None]) & flat[None, :], 1, 0), axis=1
    )
    ids = jnp.sum(
        jnp.where((before[None, :] == index[:, None]) & flat[None, :], index[None, :], 0), axis=1
    ).astype(jnp.int32)
    number = jnp.sum(flat.astype(jnp.int32)).reshape(1)

    smem = pl.BlockSpec(memory_space=pltpu.SMEM)
    vmem = pl.BlockSpec(memory_space=pltpu.VMEM)
    anywhere = pl.BlockSpec(memory_space=pl.ANY)
    guess = places // 5 + 1
    held = min(places, HELD_BYTES // (BLK * unit * 2))
    params = pltpu.CompilerParams(vmem_limit_bytes=VMEM_BYTES)
    top, mass, near, far = pl.pallas_call(
        functools.partial(table_kernel, unit, cols, held),
        out_shape=(
            jax.ShapeDtypeStruct((cols, row_count), jnp.float32),
            jax.ShapeDtypeStruct((cols, row_count), jnp.float32),
            pltpu.VMEM((held, BLK, unit), jnp.bfloat16),
            jax.ShapeDtypeStruct((max(places - held, 1), BLK, unit), jnp.bfloat16),
        ),
        in_specs=[smem, smem, vmem, vmem],
        out_specs=(vmem, vmem, vmem, anywhere),
        scratch_shapes=[pltpu.VMEM((BLK, unit), jnp.bfloat16)] * 2
        + [pltpu.VMEM((BLK, unit), jnp.float32)] * 2
        + [pltpu.VMEM((1, unit), jnp.float32)] * 2
        + [pltpu.SemaphoreType.DMA((2,))],
        compiler_params=pltpu.CompilerParams(vmem_limit_bytes=TABLE_BYTES),
        cost_estimate=pl.CostEstimate(
            flops=guess * BLK * unit * emb_width * 2,
            bytes_accessed=guess * BLK * unit,
            transcendentals=guess * BLK * unit,
        ),
        name="table",
    )(ids, number, src_rows, dst_emb)
    near = pltpu.with_memory_space_constraint(near, pltpu.VMEM)

    vocab_slice = word_table.shape[0]
    local_ids = tokens.reshape(-1) - dst_place * vocab_slice
    onehot = (local_ids[:, None] == jnp.arange(vocab_slice, dtype=jnp.int32)[None, :]).astype(
        jnp.bfloat16
    )
    looked = jnp.dot(onehot, word_table, preferred_element_type=jnp.float32)
    word_rows = lax.psum(looked.astype(jnp.bfloat16), "dst")
    logits = lax.dot_general(
        word_rows, out_emb, (((1,), (1,)), ((), ())), preferred_element_type=jnp.float32
    )
    emission = jnp.exp(logits - log_norm[None, :]).reshape(STEPS, traces, col_count)
    lines = {"src": src_count, "dst": dst_count}

    def f32(*shape):
        return jax.ShapeDtypeStruct(shape, jnp.float32)

    def room(*shape, dtype=jnp.float32):
        return pltpu.VMEM(shape, dtype)

    half = functools.partial(room, dtype=jnp.bfloat16)
    on_src = pltpu.SemaphoreType.DMA((src_count,))
    on_dst = pltpu.SemaphoreType.DMA((dst_count,))
    factor, alpha_rows = pl.pallas_call(
        functools.partial(stats_kernel, lines, piece),
        out_shape=(f32(cols, row_count), f32(traces, row_count)),
        in_specs=[vmem] * 4,
        out_specs=(vmem,) * 2,
        scratch_shapes=[
            room(dst_count, 1, piece),
            room(dst_count, 1, piece),
            room(1, piece),
            room(dst_count, 1, piece),
            half(dst_count, traces, piece),
        ]
        + [on_dst] * 6,
        compiler_params=pltpu.CompilerParams(
            collective_id=0, has_side_effects=True, vmem_limit_bytes=VMEM_BYTES
        ),
        name="stats",
    )(top, mass, alpha_moved.astype(jnp.bfloat16), near)

    lanes = -(-cols // LANES) * LANES

    def sweep(kind, alphas, weights):
        outs = [f32(traces, col_count), f32(traces, row_count)]
        if kind:
            outs.append(f32(kind, units, traces, lanes))
        return pl.pallas_call(
            functools.partial(sweep_kernel, unit, cols, held, traces, kind),
            out_shape=tuple(outs),
            in_specs=[smem, smem] + [vmem] * (len(alphas) + 2 + len(weights)) + [anywhere],
            out_specs=(vmem,) * len(outs),
            scratch_shapes=[
                pltpu.VMEM((DEPTH, BLK, unit), jnp.bfloat16),
                pltpu.SemaphoreType.DMA((DEPTH,)),
            ],
            compiler_params=params,
            cost_estimate=pl.CostEstimate(
                flops=guess * BLK * unit * traces * 4,
                bytes_accessed=guess * BLK * unit,
                transcendentals=0,
            ),
            name="sweep%d" % kind,
        )(ids, number, *alphas, factor, *weights, near, far)

    def exchange(ahead, behind, glow, glow_next):
        width = piece + LANES
        return pl.pallas_call(
            functools.partial(exchange_kernel, lines, piece, states),
            out_shape=(
                f32(traces, row_count),
                jax.ShapeDtypeStruct((traces, col_count), jnp.bfloat16),
            ),
            in_specs=[vmem] * 5,
            out_specs=(vmem, vmem),
            scratch_shapes=[
                half(src_count, traces, width),
                half(dst_count, traces, width),
                half(src_count, traces, width),
                half(dst_count, traces, width),
                half(traces, width),
                half(traces, width),
                half(dst_count, traces, width),
                half(src_count, traces, width),
            ]
            + [on_src, on_dst, on_src, on_dst, on_dst, on_src, on_dst, on_src],
            compiler_params=pltpu.CompilerParams(
                collective_id=1, has_side_effects=True, vmem_limit_bytes=VMEM_BYTES
            ),
            name="exchange",
        )(ahead, behind, glow, glow_next, near)

    last_weights = (emission[2] * beta_end).astype(jnp.bfloat16)
    pred, carried = sweep(0, [alpha_rows], [last_weights])
    alpha_1, weights_2 = exchange(pred, carried, emission[0], emission[1])
    pred, carried, middle_terms = sweep(1, [alpha_1], [weights_2])
    alpha_2, weights_1 = exchange(pred, carried, emission[1], emission[0])
    pred, carried, end_terms = sweep(2, [alpha_2, alpha_rows], [weights_1, last_weights])

    mask_rows = block_mask.shape[0]
    all_state = (
        (unit_index[None, :] // per_piece) * col_count
        + jnp.arange(src_count, dtype=jnp.int32)[:, None] * piece
        + (unit_index[None, :] % per_piece) * unit
    )
    row_block = src_place * mask_rows + jnp.arange(mask_rows, dtype=jnp.int32)
    chosen = (all_state // BLK)[:, None, :] == row_block[None, :, None]
    norm = mask_rows * src_count * cols * dst_count / (STEPS * traces)
    alpha_end, beta_start, block_counts = pl.pallas_call(
        functools.partial(final_kernel, lines, piece, states, norm),
        out_shape=(
            f32(traces, col_count), f32(traces, row_count), f32(mask_rows, lanes),
        ),
        in_specs=[vmem] * 6,
        out_specs=(vmem,) * 3,
        scratch_shapes=[
            room(src_count, traces, piece),
            room(src_count, traces, piece),
            room(traces, piece),
            room(src_count, traces, piece),
            room(dst_count, traces, piece),
            room(dst_count, traces, piece),
            room(traces, piece),
            room(traces, piece),
            room(dst_count, traces, piece),
            room(2 + STEPS, traces, LANES),
            room(src_count, 2 + STEPS, traces, LANES),
            room(2 + STEPS, traces, LANES),
            room(dst_count, 2 + STEPS, traces, LANES),
            room(units, lanes),
            room(src_count, units, lanes),
        ]
        + [on_src, on_src, on_dst, on_dst, on_src, on_src, on_dst, on_dst, on_src, on_src]
        + [pltpu.SemaphoreType.DMA((2,)), on_src, on_src, on_dst, on_dst],
        compiler_params=pltpu.CompilerParams(
            collective_id=2, has_side_effects=True, vmem_limit_bytes=VMEM_BYTES
        ),
        name="final",
    )(pred, carried, emission[2], middle_terms, end_terms, chosen.astype(jnp.float32))
    return (alpha_end, beta_start, block_counts[:, :cols])


def solution(mesh):
    return jax.shard_map(
        local,
        mesh=mesh,
        in_specs=(
            P("src", None),
            P("dst", None),
            P("dst", None),
            P("dst", None),
            P("dst"),
            P("src", "dst"),
            P(),
            P(None, "src"),
            P(None, "dst"),
        ),
        out_specs=(P(None, "dst"), P(None, "src"), P("src", "dst")),
        check_vma=False,
    )
```

time: 429 us -> 303 us (0.71)
  blocking collectives: 83.6 us -> 40.6 us
  other arithmetic: 33 us -> 4.04 us
  Pallas kernels: 237 us -> 210 us
  waiting for transfers between devices: 24 us -> 6.81 us
  starting transfers between devices: 22 us -> 12 us
    all_gather x3 -> x0, blocking collectives: 43.1 us -> none  [the longest x1 18.9 us: local(): alpha_rows = lax.all_gather(alpha_moved, 'dst', axis=1, tiled=True)]
    pallas_call x7 -> x8, Pallas kernels: 237 us -> 210 us  [the longest x3 79.1 us: sweep(): pl.pallas_call(functools.partial(sweep_kernel, unit, cols, held, traces,...]
    all_gather x2 -> x0, waiting for transfers between devices: 15.3 us -> none  [the longest x1 15.3 us: local(): pairs = lax.all_gather(jnp.stack([row_best, row_mass]), 'dst', axis=0)]
    reduce_sum x14 -> x0, other arithmetic: 11.5 us -> none  [the longest x2 2.63 us: exchange(): jnp.sum(behind, axis=1)]
    concatenate x6 -> x0, other arithmetic: 6.67 us -> none  [the longest x4 5.24 us: payload(): jnp.concatenate([value.reshape(traces, number, piece).transpose(1, 0, 2),...]
    ppermute x1 -> x0, starting transfers between devices: 6.3 us -> none  [local(): back = lax.ppermute(part, both, [(b, a) for a, b in moves])]
    unnamed x29 -> x22, local copies, waits for them, and re-layouts: 1.17 us -> 6.61 us
  transfers between devices with their start and end apart: 7 -> 3, of which waited for: 4 -> 1; matrix products, arithmetic and copies ran while one was open for 4% -> 3% of each run, Pallas kernels for 18% -> 16%
where the time goes in v1:
time: 303 us; the launch traced here: 300 us
  Pallas kernels  210 us (69%)
  blocking collectives  40.6 us (13%)
  between operations  14.3 us (5%)
  starting transfers between devices  12 us (4%)
  local copies, waits for them, and re-layouts  8.88 us (3%)
  waiting for transfers between devices  6.81 us (2%)
  other arithmetic  4.04 us (1%)
  matrix products  3.51 us (1%)
    pallas_call x3, Pallas kernels, sweep(): pl.pallas_call(functools.partial(sweep_kernel, unit, cols, held, traces,...  79.1 us
    pallas_call x1, Pallas kernels, local(): pl.pallas_call(functools.partial(table_kernel, unit, cols, held), out_sha...  47.1 us
    pallas_call x2, Pallas kernels, exchange(): pl.pallas_call(functools.partial(exchange_kernel, lines, piece, states),...  34.7 us
    pallas_call x1, Pallas kernels, local(): pl.pallas_call(functools.partial(final_kernel, lines, piece, states, norm...  30.3 us
    all_gather x1, blocking collectives, local(): whole_mask = lax.all_gather(block_mask, 'src', axis=0, tiled=True)  24.2 us
    pallas_call x1, Pallas kernels, local(): pl.pallas_call(functools.partial(stats_kernel, lines, piece), out_shape=(...  19 us
    psum x1, blocking collectives, local(): word_rows = lax.psum(looked.astype(jnp.bfloat16), 'dst')  16.4 us
    ppermute x1, starting transfers between devices, local(): alpha_moved = lax.ppermute(alpha_piece, both, moves)  7.38 us
  transfers between devices with their start and end apart: 3, of which 1 were waited for; matrix products, arithmetic and copies ran while one was open for 3% of the time, Pallas kernels for 16%

profile of v1, /device:TPU:1, one launch (start us, length us, event | category | flops | bytes accessed | tf_op | source)
XLA Modules:
  0.0 300.3 jit_solution(14667020127007554471)
XLA Ops:
  7.2 0.0 copy-start
  7.2 0.0 copy-start.7
  7.2 0.0 all-gather.3.cloned.1.call-start
  7.2 1.2 constant_dynamic-slice_fusion
  8.5 4.6 %collective-permute-start = (bf16[2048,128]{1,0:T(8,128)(2,1)S(1)}, bf16[2048,128]{1,0:T(8,128)(2,1)S(1)}, u32[]{:S(2)}, u32[]{:S(2)}) collective-permute-start(bf16[2048,128]{1,0:T(8,128)(2,1)S(1)} %constant_dynamic-slice_fusion), channel_id=1, source_target_pairs={{0,0},{4,1},{8,2},{12,3},{16,4},{20,5},{24,6},{28,7},{1,8},{5,9},{... | collective-permute-start | bytes 1572872 | tf_op jit(solution)/shard_map/ppermute | solution.py:513
  13.1 6.8 %collective-permute-done = bf16[2048,128]{1,0:T(8,128)(2,1)S(1)} collective-permute-done((bf16[2048,128]{1,0:T(8,128)(2,1)S(1)}, bf16[2048,128]{1,0:T(8,128)(2,1)S(1)}, u32[]{:S(2)}, u32[]{:S(2)}) %collective-permute-start) | collective-permute-done | bytes 524320 | tf_op jit(solution)/shard_map/ppermute | solution.py:513
  19.9 0.8 copy-done.6
  20.7 0.0 all-gather.3.cloned.1.call-update
  20.7 0.9 constant_dynamic-slice_fusion.1
  21.5 7.4 %collective-permute-start.1 = (bf16[8,2048]{1,0:T(8,128)(2,1)S(1)}, bf16[8,2048]{1,0:T(8,128)(2,1)S(1)}, u32[]{:S(2)}, u32[]{:S(2)}) collective-permute-start(bf16[8,2048]{1,0:T(8,128)(2,1)S(1)} %constant_dynamic-slice_fusion.1), channel_id=1, source_target_pairs={{0,0},{4,1},{8,2},{12,3},{16,4},{20,5},{24,6},{28,7},{1,8},{5,9},{... | collective-permute-start | bytes 98312 | tf_op jit(solution)/shard_map/ppermute | solution.py:519
  28.9 24.2 %all-gather = s32[4,32,16]{1,2,0:T(8,128)S(1)} all-gather(s32[1,32,16]{1,2,0:T(8,128)} %bitcast.9), channel_id=1, replica_groups=mesh['src'=4,'dst'=8] {'src'}, dimensions={0}, use_global_device_ids=true | all-gather | bytes 10240 | tf_op jit(solution)/shard_map/all_gather | solution.py:521
  53.2 0.1 reshape.212
  53.3 0.1 iota_compare_fusion.4
  53.3 0.6 select_reduce_fusion.2
  54.0 0.6 convert_reduce_fusion
  54.6 0.1 eq.78
  54.7 0.7 broadcast_subtract_fusion
  55.3 0.1 sub.47
  55.4 1.5 convolution_convert_fusion
  57.0 16.4 %psum.7 = bf16[24,128]{1,0:T(8,128)(2,1)S(1)} all-reduce(bf16[24,128]{1,0:T(8,128)(2,1)S(1)} %convolution_convert_fusion), channel_id=1, replica_groups=mesh['src'=4,'dst'=8] {'dst'}, use_global_device_ids=true, to_apply=%region_4.5 | all-reduce | flops 3072 | bytes 12288 | tf_op jit(solution)/shard_map/psum | solution.py:576
  73.4 0.2 select_reduce_fusion.1
  73.6 0.9 select_reduce_fusion.ids
  74.4 0.1 add_select_fusion
  74.5 0.1 compare_convert_fusion.owner
  74.6 0.0 copy-done
  74.6 2.0 fusion
  76.6 0.8 fusion.9
  77.4 47.1 %table.1 = (f32[16,16384]{1,0:T(8,128)}, f32[16,16384]{1,0:T(8,128)}, bf16[80,512,512]{2,1,0:T(8,128)(2,1)S(1)}, bf16[432,512,512]{2,1,0:T(8,128)(2,1)}) custom-call(s32[512]{0:T(512)} %select_reduce_fusion.ids, s32[1]{0:T(128)} %bitcast.1.count, bf16[16384,128]{1,0:T(8,128)(2,1)} %all-gather.3.cloned.1.call-done.src, bf16[8192,128]{1,0:T(8,128)(2,1)} %dst.1), custom_call_target="tpu_custom_call" | custom-call | flops 6912212992 | bytes 27000832 | tf_op jit(solution)/shard_map/table/pallas_call | solution.py:546
  124.6 0.0 collective-permute-done.1.alpha
  124.6 0.0 copy-start.8
  124.6 0.6 copy-done.8
  125.2 19.0 %stats.1 = (f32[16,16384]{1,0:T(8,128)}, f32[8,16384]{1,0:T(8,128)}) custom-call(f32[16,16384]{1,0:T(8,128)} %get-tuple-element.24.top, f32[16,16384]{1,0:T(8,128)} %get-tuple-element.25.mass, bf16[8,2048]{1,0:T(8,128)(2,1)} %copy-done.8, bf16[80,512,512]{2,1,0:T(8,128)(2,1)S(1)} %get-tuple-element.26.near.refs_3_.refs_5_), custom_call_target="tpu_custom_call" | custom-call | tf_op jit(solution)/shard_map/stats/pallas_call | solution.py:592
  144.2 25.1 %sweep0.1 = (f32[8,8192]{1,0:T(8,128)}, f32[8,16384]{1,0:T(8,128)}) custom-call(s32[512]{0:T(512)} %select_reduce_fusion.ids, s32[1]{0:T(128)} %bitcast.1.count, f32[8,16384]{1,0:T(8,128)} %get-tuple-element.27.refs_0_.refs_1_, f32[16,16384]{1,0:T(8,128)} %get-tuple-element.28.refs_1_.refs_2_, bf16[8,8192]{1,0:T(8,128)(2,1)} %get-tuple-element.60.refs_2_.refs_4_, ...), custom_call_target="tpu_custom_call" | custom-call | flops 864026624 | bytes 27000832 | tf_op jit(solution)/shard_map/sweep0/pallas_call | solution.py:617
  169.2 17.8 %exchange.2 = (f32[8,16384]{1,0:T(8,128)}, bf16[8,8192]{1,0:T(8,128)(2,1)}) custom-call(f32[8,8192]{1,0:T(8,128)} %get-tuple-element.30.pred, f32[8,16384]{1,0:T(8,128)} %get-tuple-element.31.carried, f32[8,8192]{1,0:T(8,128)} %get-tuple-element.62.glow.glow_next, f32[8,8192]{1,0:T(8,128)} %get-tuple-element.61.glow_next.glow, ...), custom_call_target="tpu_custom_call" | custom-call | tf_op jit(solution)/shard_map/exchange/pallas_call | solution.py:637
  187.1 26.9 %sweep1.1 = (f32[8,8192]{1,0:T(8,128)}, f32[8,16384]{1,0:T(8,128)}, f32[1,32,8,128]{3,2,1,0:T(8,128)}) custom-call(s32[512]{0:T(512)} %select_reduce_fusion.ids, s32[1]{0:T(128)} %bitcast.1.count, f32[8,16384]{1,0:T(8,128)} %get-tuple-element.32.refs_0_, f32[16,16384]{1,0:T(8,128)} %get-tuple-element.28.refs_1_.refs_2_, ...), custom_call_target="tpu_custom_call" | custom-call | flops 864026624 | bytes 27000832 | tf_op jit(solution)/shard_map/sweep1/pallas_call | solution.py:617
  213.9 16.9 %exchange.3 = (f32[8,16384]{1,0:T(8,128)}, bf16[8,8192]{1,0:T(8,128)(2,1)}) custom-call(f32[8,8192]{1,0:T(8,128)} %get-tuple-element.34.pred, f32[8,16384]{1,0:T(8,128)} %get-tuple-element.35.carried, f32[8,8192]{1,0:T(8,128)} %get-tuple-element.61.glow_next.glow, f32[8,8192]{1,0:T(8,128)} %get-tuple-element.62.glow.glow_next, ...), custom_call_target="tpu_custom_call" | custom-call | tf_op jit(solution)/shard_map/exchange/pallas_call | solution.py:637
  230.8 0.0 copy-start.5
  230.8 0.0 copy-start.1
  230.8 27.2 %sweep2.1 = (f32[8,8192]{1,0:T(8,128)}, f32[8,16384]{1,0:T(8,128)}, f32[2,32,8,128]{3,2,1,0:T(8,128)}) custom-call(s32[512]{0:T(512)} %select_reduce_fusion.ids, s32[1]{0:T(128)} %bitcast.1.count, f32[8,16384]{1,0:T(8,128)} %get-tuple-element.36.refs_0_, f32[8,16384]{1,0:T(8,128)} %get-tuple-element.27.refs_0_.refs_1_, ...), custom_call_target="tpu_custom_call" | custom-call | flops 864026624 | bytes 27000832 | tf_op jit(solution)/shard_map/sweep2/pallas_call | solution.py:617
  258.0 0.0 copy-done.5
  258.0 0.0 copy-start.2
  258.1 1.0 copy-done.2
  259.1 0.9 copy-done.3
  260.0 0.9 copy-done.4
  261.0 30.3 %final.1 = (f32[8,8192]{1,0:T(8,128)S(1)}, f32[8,16384]{1,0:T(8,128)S(1)}, f32[32,128]{1,0:T(8,128)S(1)}) custom-call(f32[8,8192]{1,0:T(8,128)S(1)} %copy-done.3, f32[8,16384]{1,0:T(8,128)S(1)} %copy-done.2, f32[8,8192]{1,0:T(8,128)S(1)} %get-tuple-element.59.glow, f32[1,32,8,128]{3,2,1,0:T(8,128)S(1)} %copy-done.5, f32[2,32,8,128]{3,2,1,0:T(8,128)S(1)} %copy-done.4, ...), custom_call_target="tpu_custom_call" | custom-call | tf_op jit(solution)/shard_map/final/pallas_call | solution.py:678
  291.3 0.7 copy.20
  292.0 0.7 copy.23
  292.7 0.8 copy.24
  (11 shorter events, 0.1 us)
Async XLA Ops:
  7.2 67.4 %copy-start = (bf16[8192,128]{1,0:T(8,128)(2,1)S(1)}, bf16[8192,128]{1,0:T(8,128)(2,1)}, u32[]{:S(2)}) copy-start(bf16[8192,128]{1,0:T(8,128)(2,1)} %param.11) | copy-start | bytes 6291460
  7.2 69.4 %copy-start.7 = (f32[8,8192]{1,0:T(8,128)S(1)}, f32[8,8192]{1,0:T(8,128)}, u32[]{:S(2)}) copy-start(f32[8,8192]{1,0:T(8,128)} %param.17) | copy-start | bytes 786436
  7.2 70.2 %all-gather.3.cloned.1.call-start = ((), (), s32[]{:S(2)}) async-start(), calls=%async_computation | async-start | bytes 4718592 | tf_op jit(solution)/shard_map/all_gather | solution.py:514
  8.5 11.4 %collective-permute-start = (bf16[2048,128]{1,0:T(8,128)(2,1)S(1)}, bf16[2048,128]{1,0:T(8,128)(2,1)S(1)}, u32[]{:S(2)}, u32[]{:S(2)}) collective-permute-start(bf16[2048,128]{1,0:T(8,128)(2,1)S(1)} %constant_dynamic-slice_fusion), channel_id=1, source_target_pairs={{0,0},{4,1},{8,2},{12,3},{16,4},{20,5},{24,6},{28,7},{1,8},{5,9},{... | collective-permute-start | bytes 1572872 | tf_op jit(solution)/shard_map/ppermute | solution.py:513
  19.9 0.8 copy-start.6
  21.5 103.0 %collective-permute-start.1 = (bf16[8,2048]{1,0:T(8,128)(2,1)S(1)}, bf16[8,2048]{1,0:T(8,128)(2,1)S(1)}, u32[]{:S(2)}, u32[]{:S(2)}) collective-permute-start(bf16[8,2048]{1,0:T(8,128)(2,1)S(1)} %constant_dynamic-slice_fusion.1), channel_id=1, source_target_pairs={{0,0},{4,1},{8,2},{12,3},{16,4},{20,5},{24,6},{28,7},{1,8},{5,9},{... | collective-permute-start | bytes 98312 | tf_op jit(solution)/shard_map/ppermute | solution.py:519
  124.6 0.6 copy-start.8
  230.8 27.2 %copy-start.5 = (f32[1,32,8,128]{3,2,1,0:T(8,128)S(1)}, f32[1,32,8,128]{3,2,1,0:T(8,128)}, u32[]{:S(2)}) copy-start(f32[1,32,8,128]{3,2,1,0:T(8,128)} %get-tuple-element.40.mid_terms) | copy-start | bytes 393220
  230.8 62.7 %copy-start.1 = (bf16[8192,128]{1,0:T(8,128)(2,1)S(1)}, bf16[8192,128]{1,0:T(8,128)(2,1)}, u32[]{:S(2)}) copy-start(bf16[8192,128]{1,0:T(8,128)(2,1)} %param.11) | copy-start | bytes 6291460
  258.0 1.0 copy-start.2
  259.1 0.9 copy-start.3
  260.0 0.9 copy-start.4
Sparse Core Ops, SparseCore 0:
  20.8 55.5 all-gather.2

commit v2 on v1

--- a/solution.py
+++ b/solution.py
@@ -23,6 +23,7 @@
     buf_0, buf_1, scores_0, scores_1, best_0, best_1, sems,
 ):
     number = count[0]
+    src = src.reshape(top.shape[1], src.shape[-1])
     chunk = min(128, unit)
     pieces = unit // chunk
     top[...] = jnp.full_like(top, very_negative)
@@ -241,6 +242,139 @@
             copy.start()
             copies.append(copy)
         return copies
+
+
+def gather_kernel(
+    lines, group, piece, states, source, mask, looked, out_emb, log_norm, start,
+    rows, masks, emission, moved, land_w, local_sems, alpha_sems, *sems,
+):
+    net = Lines(lines)
+    net.greet()
+    src, dst = lines["src"], lines["dst"]
+    z, d = net.place["src"], net.place["dst"]
+    chips = dst // 2
+    sibling = d + 1 - 2 * lax.rem(d, 2)
+    held = z * dst + d
+    to_dst, to_src = lax.div(held, src), lax.rem(held, src)
+    number = d * src + z
+    from_src, from_dst = lax.div(number, dst), lax.rem(number, dst)
+    away = (to_src != z) | (to_dst != d)
+    barrier = pltpu.get_barrier_semaphore()
+    mesh_ids = pl.DeviceIdType.MESH
+    mine = start.at[:, pl.ds(pl.multiple_of(d * piece, piece), piece)]
+
+    @pl.when(away)
+    def _():
+        for s, t in ((to_src, to_dst), (from_src, from_dst)):
+            pl.semaphore_signal(
+                barrier, inc=1, device_id={"src": s, "dst": t}, device_id_type=mesh_ids
+            )
+        net.gather_in(2)
+
+    @pl.when(jnp.logical_not(away))
+    def _():
+        net.gather_in()
+
+    def plane(value):
+        return pl.ds(value * group, group)
+
+    def pass_on(source_ref, target_ref, send, recv, device):
+        copy = pltpu.make_async_remote_copy(
+            src_ref=source_ref, dst_ref=target_ref, send_sem=send, recv_sem=recv,
+            device_id=device, device_id_type=mesh_ids,
+        )
+        copy.start()
+        return copy
+
+    along = []
+    for k in range(1, src):
+        other = net.peer("src", k)
+        along.append(
+            pass_on(
+                source.at[:, other, d], rows.at[plane(z), d],
+                sems[0].at[k], sems[1].at[k], {"src": other},
+            )
+        )
+    words = net.send("dst", lambda peer: looked, land_w, sems[2], sems[3])
+    masks[z] = mask[...]
+    marks = [
+        pass_on(
+            mask, masks.at[z], sems[4].at[k], sems[5].at[k], {"src": net.peer("src", k)}
+        )
+        for k in range(1, src)
+    ]
+    move = pltpu.make_async_remote_copy(
+        src_ref=mine, dst_ref=moved, send_sem=alpha_sems.at[0], recv_sem=alpha_sems.at[1],
+        device_id={"src": to_src, "dst": to_dst}, device_id_type=mesh_ids,
+    )
+    stay = pltpu.make_async_copy(mine, moved, alpha_sems.at[2])
+
+    @pl.when(away)
+    def _():
+        move.start()
+
+    @pl.when(jnp.logical_not(away))
+    def _():
+        stay.start()
+
+    own = pltpu.make_async_copy(source.at[:, z], rows.at[plane(z)], local_sems)
+    own.start()
+
+    across, beside = [], []
+    for k in range(1, src):
+        along[k - 1].wait_recv()
+        here = plane(net.origin("src", k))
+        block = rows.at[here, d]
+        for m in range(1, chips):
+            across.append(
+                pass_on(
+                    block, block, sems[6].at[k, m], sems[7].at[k, m],
+                    {"dst": lax.rem(d + 2 * m, dst)},
+                )
+            )
+        beside.append(
+            pass_on(block, block, sems[8].at[k, 0], sems[9].at[k, 0], {"dst": sibling})
+        )
+        if k == 1:
+            total = looked[...].astype(jnp.float32)
+            for w in range(1, dst):
+                words[w - 1].wait_recv()
+                total = total + land_w[w].astype(jnp.float32)
+            total = total.astype(jnp.bfloat16)
+            cols = out_emb.shape[0]
+            width = min(cols, 1024)
+            for c in range(0, cols, width):
+                logits = lax.dot_general(
+                    total, out_emb[c:c + width, :], (((1,), (1,)), ((), ())),
+                    preferred_element_type=jnp.float32,
+                )
+                emission[:, c:c + width] = jnp.exp(logits - log_norm[:, c:c + width])
+    for k in range(1, src):
+        here = plane(net.origin("src", k))
+        for m in range(1, chips):
+            across[(k - 1) * (chips - 1) + m - 1].wait_recv()
+            block = rows.at[here, lax.rem(d + dst - 2 * m, dst)]
+            beside.append(
+                pass_on(block, block, sems[8].at[k, m], sems[9].at[k, m], {"dst": sibling})
+            )
+    own.wait()
+    for copy in marks:
+        copy.wait_recv()
+
+    @pl.when(away)
+    def _():
+        move.wait_recv()
+        move.wait_send()
+
+    @pl.when(jnp.logical_not(away))
+    def _():
+        stay.wait()
+
+    for copy in beside:
+        copy.wait_recv()
+    for copies in (along, words, marks, across, beside):
+        for copy in copies:
+            copy.wait_send()
 
 
 def stats_kernel(
@@ -499,26 +633,63 @@
     units = row_count // unit
     cols = col_count // BLK
     places = units * cols
-    padded = -(-places // LANES) * LANES
     src_place = lax.axis_index("src")
     dst_place = lax.axis_index("dst")
-    both = ("src", "dst")
-    moves = [
-        ((d // group) * dst_count + (d % group) * src_count + z, z * dst_count + d)
-        for z in range(src_count)
-        for d in range(dst_count)
-    ]
-
-    def spread_rows(mine):
-        moved = lax.ppermute(mine, both, moves)
-        return lax.all_gather(moved, "dst", axis=0, tiled=True)
-
-    mine = lax.dynamic_slice_in_dim(src_emb, dst_place * piece, piece, 0)
-    src_rows = spread_rows(mine)
-    alpha_piece = lax.dynamic_slice_in_dim(alpha_start, dst_place * piece, piece, 1)
-    alpha_moved = lax.ppermute(alpha_piece, both, moves)
-
-    whole_mask = lax.all_gather(block_mask, "src", axis=0, tiled=True)
+    smem = pl.BlockSpec(memory_space=pltpu.SMEM)
+    vmem = pl.BlockSpec(memory_space=pltpu.VMEM)
+    anywhere = pl.BlockSpec(memory_space=pl.ANY)
+    hbm = pl.BlockSpec(memory_space=pltpu.HBM)
+    lines = {"src": src_count, "dst": dst_count}
+    on_src = pltpu.SemaphoreType.DMA((src_count,))
+    on_dst = pltpu.SemaphoreType.DMA((dst_count,))
+    on_chips = pltpu.SemaphoreType.DMA((src_count, dst_count // 2))
+
+    def f32(*shape):
+        return jax.ShapeDtypeStruct(shape, jnp.float32)
+
+    def room(*shape, dtype=jnp.float32):
+        return pltpu.VMEM(shape, dtype)
+
+    half = functools.partial(room, dtype=jnp.bfloat16)
+
+    vocab_slice = word_table.shape[0]
+    local_ids = tokens.reshape(-1) - dst_place * vocab_slice
+    onehot = (local_ids[:, None] == jnp.arange(vocab_slice, dtype=jnp.int32)[None, :]).astype(
+        jnp.bfloat16
+    )
+    looked = jnp.dot(onehot, word_table, preferred_element_type=jnp.float32)
+    share = piece // dst_count
+    gathered, masks, emission, alpha_moved = pl.pallas_call(
+        functools.partial(gather_kernel, lines, group, piece, states),
+        out_shape=(
+            half(dst_count, dst_count, share, emb_width),
+            jax.ShapeDtypeStruct((src_count,) + block_mask.shape, jnp.int32),
+            f32(STEPS * traces, col_count),
+            f32(traces, piece),
+        ),
+        in_specs=[hbm, vmem, vmem, vmem, vmem, hbm],
+        out_specs=(vmem,) * 4,
+        scratch_shapes=[
+            half(dst_count, STEPS * traces, emb_width),
+            pltpu.SemaphoreType.DMA,
+            pltpu.SemaphoreType.DMA((3,)),
+        ]
+        + [on_src, on_src, on_dst, on_dst, on_src, on_src]
+        + [on_chips] * 4,
+        compiler_params=pltpu.CompilerParams(
+            collective_id=3, has_side_effects=True, vmem_limit_bytes=TABLE_BYTES
+        ),
+        name="gather",
+    )(
+        pltpu.with_memory_space_constraint(
+            src_emb.reshape(group, src_count, dst_count, share, emb_width), pltpu.HBM
+        ),
+        block_mask, looked.astype(jnp.bfloat16), out_emb, log_norm[None, :],
+        pltpu.with_memory_space_constraint(alpha_start, pltpu.HBM),
+    )
+    gathered = pltpu.with_memory_space_constraint(gathered, pltpu.VMEM)
+    emission = emission.reshape(STEPS, traces, col_count)
+    whole_mask = masks.reshape(src_count * block_mask.shape[0], cols)
     unit_index = jnp.arange(units, dtype=jnp.int32)
     per_piece = piece // unit
     unit_state = (
@@ -537,9 +708,6 @@
     ).astype(jnp.int32)
     number = jnp.sum(flat.astype(jnp.int32)).reshape(1)
 
-    smem = pl.BlockSpec(memory_space=pltpu.SMEM)
-    vmem = pl.BlockSpec(memory_space=pltpu.VMEM)
-    anywhere = pl.BlockSpec(memory_space=pl.ANY)
     guess = places // 5 + 1
     held = min(places, HELD_BYTES // (BLK * unit * 2))
     params = pltpu.CompilerParams(vmem_limit_bytes=VMEM_BYTES)
@@ -564,31 +732,9 @@
             transcendentals=guess * BLK * unit,
         ),
         name="table",
-    )(ids, number, src_rows, dst_emb)
+    )(ids, number, gathered, dst_emb)
     near = pltpu.with_memory_space_constraint(near, pltpu.VMEM)
 
-    vocab_slice = word_table.shape[0]
-    local_ids = tokens.reshape(-1) - dst_place * vocab_slice
-    onehot = (local_ids[:, None] == jnp.arange(vocab_slice, dtype=jnp.int32)[None, :]).astype(
-        jnp.bfloat16
-    )
-    looked = jnp.dot(onehot, word_table, preferred_element_type=jnp.float32)
-    word_rows = lax.psum(looked.astype(jnp.bfloat16), "dst")
-    logits = lax.dot_general(
-        word_rows, out_emb, (((1,), (1,)), ((), ())), preferred_element_type=jnp.float32
-    )
-    emission = jnp.exp(logits - log_norm[None, :]).reshape(STEPS, traces, col_count)
-    lines = {"src": src_count, "dst": dst_count}
-
-    def f32(*shape):
-        return jax.ShapeDtypeStruct(shape, jnp.float32)
-
-    def room(*shape, dtype=jnp.float32):
-        return pltpu.VMEM(shape, dtype)
-
-    half = functools.partial(room, dtype=jnp.bfloat16)
-    on_src = pltpu.SemaphoreType.DMA((src_count,))
-    on_dst = pltpu.SemaphoreType.DMA((dst_count,))
     factor, alpha_rows = pl.pallas_call(
         functools.partial(stats_kernel, lines, piece),
         out_shape=(f32(cols, row_count), f32(traces, row_count)),

time: 303 us -> 262 us (0.86)
  blocking collectives: 40.6 us -> 0 us
  Pallas kernels: 210 us -> 242 us
  between operations: 14.3 us -> 0.8 us
  starting transfers between devices: 12 us -> 0 us
  waiting for transfers between devices: 6.81 us -> 0 us
  local copies, waits for them, and re-layouts: 8.88 us -> 13 us
  matrix products: 3.51 us -> 0.3 us
    pallas_call x0 -> x1, Pallas kernels: none -> 31.7 us  [local(): pl.pallas_call(functools.partial(gather_kernel, lines, group, piece, stat...]
    all_gather x1 -> x0, blocking collectives: 24.2 us -> none  [local(): whole_mask = lax.all_gather(block_mask, 'src', axis=0, tiled=True)]
    psum x1 -> x0, blocking collectives: 16.4 us -> none  [local(): word_rows = lax.psum(looked.astype(jnp.bfloat16), 'dst')]
    ppermute x2 -> x0, starting transfers between devices: 12 us -> none  [the longest x1 7.38 us: local(): alpha_moved = lax.ppermute(alpha_piece, both, moves)]
    ppermute x2 -> x0, waiting for transfers between devices: 6.8 us -> none  [the longest x1 6.79 us: spread_rows(): moved = lax.ppermute(mine, both, moves)]
    unnamed x22 -> x26, local copies, waits for them, and re-layouts: 6.61 us -> 12.8 us
  transfers between devices with their start and end apart: 3 -> 0, of which waited for: 1 -> 0; matrix products, arithmetic and copies ran while one was open for 3% -> 0% of each run, Pallas kernels for 16% -> 0%
where the time goes in v2:
time: 262 us; the launch traced here: 261 us
  Pallas kernels  242 us (92%)
  local copies, waits for them, and re-layouts  13 us (5%)
  other arithmetic  4.85 us (2%)
    pallas_call x3, Pallas kernels, sweep(): pl.pallas_call(functools.partial(sweep_kernel, unit, cols, held, traces,...  78.5 us
    pallas_call x1, Pallas kernels, local(): pl.pallas_call(functools.partial(table_kernel, unit, cols, held), out_sha...  44.7 us
    pallas_call x2, Pallas kernels, exchange(): pl.pallas_call(functools.partial(exchange_kernel, lines, piece, states),...  35 us
    pallas_call x1, Pallas kernels, local(): pl.pallas_call(functools.partial(gather_kernel, lines, group, piece, stat...  31.7 us
    pallas_call x1, Pallas kernels, local(): pl.pallas_call(functools.partial(final_kernel, lines, piece, states, norm...  31.6 us
    pallas_call x1, Pallas kernels, local(): pl.pallas_call(functools.partial(stats_kernel, lines, piece), out_shape=(...  20.6 us
    unnamed x26, local copies, waits for them, and re-layouts  12.8 us

profile of v2, /device:TPU:1, one launch (start us, length us, event | category | flops | bytes accessed | tf_op | source)
XLA Modules:
  0.0 261.0 jit_solution(16594245035743432973)
XLA Ops:
  0.6 0.0 copy-start
  0.7 0.8 broadcast_subtract_fusion
  1.4 0.1 sub.39
  1.5 0.4 copy-done
  1.9 0.3 convolution_convert_fusion.looked
  2.2 0.8 copy.16.mask
  3.0 0.0 copy-start.2
  3.0 1.6 copy-done.2
  4.6 0.0 copy-start.7
  4.6 0.8 copy-done.7
  5.3 31.7 %gather.1 = (bf16[8,8,256,128]{3,2,1,0:T(8,128)(2,1)S(1)}, s32[4,32,16]{2,1,0:T(8,128)S(1)}, f32[24,8192]{1,0:T(8,128)S(1)}, f32[8,2048]{1,0:T(8,128)S(1)}) custom-call(bf16[2,4,8,256,128]{4,3,2,1,0:T(8,128)(2,1)} %bitcast.9, s32[32,16]{1,0:T(8,128)S(1)} %copy.16.mask, bf16[24,128]{1,0:T(8,128)(2,1)S(1)} %convolution_convert_fusion.looked, ...), custom_call_target="tpu_custom_call" | custom-call | tf_op jit(solution)/shard_map/gather/pallas_call | solution.py:662
  37.0 0.0 copy-start.8
  37.0 1.9 copy-done.8
  39.0 0.1 iota_compare_fusion.4
  39.1 0.6 select_reduce_fusion.2
  39.7 0.7 convert_reduce_fusion
  40.4 0.1 eq.81
  40.5 0.2 select_reduce_fusion.1
  40.7 0.9 select_reduce_fusion.ids
  41.5 0.0 copy-start.9
  41.5 2.2 copy-done.9
  43.7 44.7 %table.1 = (f32[16,16384]{1,0:T(8,128)}, f32[16,16384]{1,0:T(8,128)}, bf16[80,512,512]{2,1,0:T(8,128)(2,1)S(1)}, bf16[432,512,512]{2,1,0:T(8,128)(2,1)}) custom-call(s32[512]{0:T(512)} %select_reduce_fusion.ids, s32[1]{0:T(128)} %bitcast.3.count, bf16[8,8,256,128]{3,2,1,0:T(8,128)(2,1)S(1)} %copy-done.9, bf16[8192,128]{1,0:T(8,128)(2,1)} %dst.1), custom_call_target="tpu_custom_call" | custom-call | flops 6912212992 | bytes 27000832 | tf_op jit(solution)/shard_map/table/pallas_call | solution.py:714
  88.4 0.6 convert_element_type.19.alpha
  89.0 0.0 copy-start.10
  89.0 20.6 %stats.1 = (f32[16,16384]{1,0:T(8,128)}, f32[8,16384]{1,0:T(8,128)}) custom-call(f32[16,16384]{1,0:T(8,128)} %get-tuple-element.30.top, f32[16,16384]{1,0:T(8,128)} %get-tuple-element.31.mass, bf16[8,2048]{1,0:T(8,128)(2,1)} %convert_element_type.19.alpha, bf16[80,512,512]{2,1,0:T(8,128)(2,1)S(1)} %get-tuple-element.33.near.refs_3_.refs_5_), custom_call_target="tpu_custom_call" | custom-call | tf_op jit(solution)/shard_map/stats/pallas_call | solution.py:738
  109.6 0.0 copy-done.10
  109.6 0.8 fusion.8
  110.5 24.9 %sweep0.1 = (f32[8,8192]{1,0:T(8,128)}, f32[8,16384]{1,0:T(8,128)}) custom-call(s32[512]{0:T(512)} %select_reduce_fusion.ids, s32[1]{0:T(128)} %bitcast.3.count, f32[8,16384]{1,0:T(8,128)} %get-tuple-element.34.refs_0_.refs_1_, f32[16,16384]{1,0:T(8,128)} %get-tuple-element.35.refs_1_.refs_2_, bf16[8,8192]{1,0:T(8,128)(2,1)} %get-tuple-element.65.refs_2_.refs_4_, ...), custom_call_target="tpu_custom_call" | custom-call | flops 864026624 | bytes 27000832 | tf_op jit(solution)/shard_map/sweep0/pallas_call | solution.py:763
  135.3 17.7 %exchange.2 = (f32[8,16384]{1,0:T(8,128)}, bf16[8,8192]{1,0:T(8,128)(2,1)}) custom-call(f32[8,8192]{1,0:T(8,128)} %get-tuple-element.38.pred, f32[8,16384]{1,0:T(8,128)} %get-tuple-element.39.carried, f32[8,8192]{1,0:T(8,128)} %get-tuple-element.67.glow.glow_next, f32[8,8192]{1,0:T(8,128)} %get-tuple-element.66.glow_next.glow, ...), custom_call_target="tpu_custom_call" | custom-call | tf_op jit(solution)/shard_map/exchange/pallas_call | solution.py:783
  153.0 26.7 %sweep1.1 = (f32[8,8192]{1,0:T(8,128)}, f32[8,16384]{1,0:T(8,128)}, f32[1,32,8,128]{3,2,1,0:T(8,128)}) custom-call(s32[512]{0:T(512)} %select_reduce_fusion.ids, s32[1]{0:T(128)} %bitcast.3.count, f32[8,16384]{1,0:T(8,128)} %get-tuple-element.40.refs_0_, f32[16,16384]{1,0:T(8,128)} %get-tuple-element.35.refs_1_.refs_2_, ...), custom_call_target="tpu_custom_call" | custom-call | flops 864026624 | bytes 27000832 | tf_op jit(solution)/shard_map/sweep1/pallas_call | solution.py:763
  179.7 17.3 %exchange.3 = (f32[8,16384]{1,0:T(8,128)}, bf16[8,8192]{1,0:T(8,128)(2,1)}) custom-call(f32[8,8192]{1,0:T(8,128)} %get-tuple-element.42.pred, f32[8,16384]{1,0:T(8,128)} %get-tuple-element.43.carried, f32[8,8192]{1,0:T(8,128)} %get-tuple-element.66.glow_next.glow, f32[8,8192]{1,0:T(8,128)} %get-tuple-element.67.glow.glow_next, ...), custom_call_target="tpu_custom_call" | custom-call | tf_op jit(solution)/shard_map/exchange/pallas_call | solution.py:783
  197.1 0.0 copy-start.6
  197.1 0.0 copy-start.1
  197.1 26.9 %sweep2.1 = (f32[8,8192]{1,0:T(8,128)}, f32[8,16384]{1,0:T(8,128)}, f32[2,32,8,128]{3,2,1,0:T(8,128)}) custom-call(s32[512]{0:T(512)} %select_reduce_fusion.ids, s32[1]{0:T(128)} %bitcast.3.count, f32[8,16384]{1,0:T(8,128)} %get-tuple-element.44.refs_0_, f32[8,16384]{1,0:T(8,128)} %get-tuple-element.34.refs_0_.refs_1_, ...), custom_call_target="tpu_custom_call" | custom-call | flops 864026624 | bytes 27000832 | tf_op jit(solution)/shard_map/sweep2/pallas_call | solution.py:763
  224.1 0.1 add_select_fusion
  224.1 0.1 compare_convert_fusion.owner
  224.2 0.0 copy-done.6
  224.2 0.0 copy-start.3
  224.2 1.0 copy-done.3
  225.3 0.0 copy-start.4
  225.3 0.9 copy-done.4
  226.2 0.0 copy-start.5
  226.2 0.9 copy-done.5
  227.2 31.6 %final.1 = (f32[8,8192]{1,0:T(8,128)S(1)}, f32[8,16384]{1,0:T(8,128)S(1)}, f32[32,128]{1,0:T(8,128)S(1)}) custom-call(f32[8,8192]{1,0:T(8,128)S(1)} %copy-done.4, f32[8,16384]{1,0:T(8,128)S(1)} %copy-done.3, f32[8,8192]{1,0:T(8,128)S(1)} %get-tuple-element.64.glow, f32[1,32,8,128]{3,2,1,0:T(8,128)S(1)} %copy-done.6, f32[2,32,8,128]{3,2,1,0:T(8,128)S(1)} %copy-done.5, ...), custom_call_target="tpu_custom_call" | custom-call | tf_op jit(solution)/shard_map/final/pallas_call | solution.py:824
  258.8 0.7 copy.18
  259.5 0.7 copy.21
  260.2 0.8 copy.22
  260.9 0.0 copy-done.1
  (5 shorter events, 0.1 us)
Async XLA Ops:
  0.6 1.2 copy-start
  3.0 1.6 copy-start.2
  4.6 0.8 copy-start.7
  37.0 2.0 copy-start.8
  41.5 2.2 copy-start.9
  89.0 20.6 %copy-start.10 = (f32[8,8192]{1,0:T(8,128)S(1)}, f32[8,8192]{1,0:T(8,128)}, u32[]{:S(2)}) copy-start(f32[8,8192]{1,0:T(8,128)} %param.17) | copy-start | bytes 786436
  197.1 27.2 %copy-start.6 = (f32[1,32,8,128]{3,2,1,0:T(8,128)S(1)}, f32[1,32,8,128]{3,2,1,0:T(8,128)}, u32[]{:S(2)}) copy-start(f32[1,32,8,128]{3,2,1,0:T(8,128)} %get-tuple-element.48.mid_terms) | copy-start | bytes 393220
  197.1 63.9 %copy-start.1 = (bf16[4096,128]{1,0:T(8,128)(2,1)S(1)}, bf16[4096,128]{1,0:T(8,128)(2,1)}, u32[]{:S(2)}) copy-start(bf16[4096,128]{1,0:T(8,128)(2,1)} %param.12) | copy-start | bytes 3145732
  224.2 1.0 copy-start.3
  225.3 0.9 copy-start.4
  226.2 0.9 copy-start.5

commit v3 on v2

--- a/solution.py
+++ b/solution.py
@@ -2,6 +2,7 @@
 
 import jax
 import jax.numpy as jnp
+import numpy as np
 from jax import lax
 from jax.experimental import pallas as pl
 from jax.experimental.pallas import tpu as pltpu
@@ -13,21 +14,24 @@
 DEPTH = 8
 very_negative = -1e30
 GROUP = 4
-HELD_BYTES = 40 * 1024 * 1024
-TABLE_BYTES = 16 * 1024 * 1024
-VMEM_BYTES = 16 * 1024 * 1024
+HELD_BYTES = 48 * 1024 * 1024
+TABLE_BYTES = 14 * 1024 * 1024
+VMEM_BYTES = 14 * 1024 * 1024
 
 
 def table_kernel(
-    unit, cols, held, ids, count, src, dst, top, mass, near, far,
+    unit, cols, held, ids, count, src_far, dst_far, top, mass, near, far, src, dst, load_sems,
     buf_0, buf_1, scores_0, scores_1, best_0, best_1, sems,
 ):
     number = count[0]
+    loads = fetch([(src_far, src), (dst_far, dst)], load_sems)
     src = src.reshape(top.shape[1], src.shape[-1])
     chunk = min(128, unit)
     pieces = unit // chunk
     top[...] = jnp.full_like(top, very_negative)
     mass[...] = jnp.zeros_like(mass)
+    for copy in loads:
+        copy.wait()
 
     def place(slot):
         entry = ids[slot]
@@ -244,12 +248,24 @@
         return copies
 
 
+def fetch(pairs, sems):
+    copies = [
+        pltpu.make_async_copy(source, target, sems.at[n])
+        for n, (source, target) in enumerate(pairs)
+    ]
+    for copy in copies:
+        copy.start()
+    return copies
+
+
 def gather_kernel(
-    lines, group, piece, states, source, mask, looked, out_emb, log_norm, start,
-    rows, masks, emission, moved, land_w, local_sems, alpha_sems, *sems,
+    lines, group, piece, source, mask, looked, out_far, norm_far, end_far, start,
+    rows, masks, emission_far, last_far, moved, land_w, out_emb, log_norm, end, emission, last,
+    local_sems, alpha_sems, load_sems, *sems,
 ):
     net = Lines(lines)
     net.greet()
+    loads = fetch([(out_far, out_emb), (norm_far, log_norm), (end_far, end)], load_sems)
     src, dst = lines["src"], lines["dst"]
     z, d = net.place["src"], net.place["dst"]
     chips = dst // 2
@@ -341,6 +357,8 @@
                 words[w - 1].wait_recv()
                 total = total + land_w[w].astype(jnp.float32)
             total = total.astype(jnp.bfloat16)
+            for copy in loads:
+                copy.wait()
             cols = out_emb.shape[0]
             width = min(cols, 1024)
             for c in range(0, cols, width):
@@ -348,7 +366,11 @@
                     total, out_emb[c:c + width, :], (((1,), (1,)), ((), ())),
                     preferred_element_type=jnp.float32,
                 )
-                emission[:, c:c + width] = jnp.exp(logits - log_norm[:, c:c + width])
+                risen = jnp.exp(logits - log_norm[:, c:c + width])
+                emission[:, c:c + width] = risen
+                tail = risen[risen.shape[0] - end.shape[0]:]
+                last[:, c:c + width] = (tail * end[:, c:c + width]).astype(jnp.bfloat16)
+            stores = fetch([(emission, emission_far), (last, last_far)], load_sems)
     for k in range(1, src):
         here = plane(net.origin("src", k))
         for m in range(1, chips):
@@ -358,6 +380,8 @@
                 pass_on(block, block, sems[8].at[k, m], sems[9].at[k, m], {"dst": sibling})
             )
     own.wait()
+    for copy in stores:
+        copy.wait()
     for copy in marks:
         copy.wait_recv()
 
@@ -379,11 +403,12 @@
 
 def stats_kernel(
     lines, piece, top, mass, alpha, near, factor, spread_alpha,
-    parts, land, merged, land_2, land_a, *sems,
+    parts, land, merged, land_2, own, land_a, *sems,
 ):
     net = Lines(lines)
     net.greet()
     count = lines["dst"]
+    own[...] = alpha[...].astype(jnp.bfloat16)
     for p in range(count):
         rows = slice(p * piece, (p + 1) * piece)
         best = jnp.max(top[:, rows], axis=0, keepdims=True)
@@ -393,7 +418,7 @@
         )
     net.gather_in()
     first = net.send("dst", lambda peer: parts.at[peer], land, sems[0], sems[1])
-    sent = net.send("dst", lambda peer: alpha, land_a, sems[4], sems[5])
+    sent = net.send("dst", lambda peer: own, land_a, sems[4], sems[5])
     land[0] = parts[net.place["dst"]]
     for copy in first:
         copy.wait_recv()
@@ -415,7 +440,7 @@
         rows = pl.ds(pl.multiple_of(net.origin("dst", k) * piece, piece), piece)
         if k:
             sent[k - 1].wait_recv()
-        spread_alpha[:, rows] = (alpha[...] if k == 0 else land_a[k]).astype(jnp.float32)
+        spread_alpha[:, rows] = (own[...] if k == 0 else land_a[k]).astype(jnp.float32)
     for k in range(1, count):
         second[k - 1].wait_recv()
         finish(k, land_2[k])
@@ -424,11 +449,24 @@
 
 
 def exchange_kernel(
-    lines, piece, states, pred, carried, glow, glow_next, near, alpha, weights,
+    lines, piece, states, step, later, pred_far, carried_far, emission, near, alpha, weights,
+    pred, carried, glow, glow_next, load_sems,
     out_f, out_b, in_f, in_b, red_f, red_b, land_f, land_b, *sems,
 ):
     net = Lines(lines)
+    traces = pred.shape[0]
     net.greet()
+    loads = fetch(
+        [
+            (pred_far, pred),
+            (emission.at[pl.ds(step * traces, traces)], glow),
+            (carried_far, carried),
+            (emission.at[pl.ds(later * traces, traces)], glow_next),
+        ],
+        load_sems,
+    )
+    for copy in loads:
+        copy.wait()
     shape = (pred.shape[0], LANES)
     total_f = jnp.broadcast_to(
         jnp.sum(pred[...] * glow[...], axis=1, keepdims=True), shape
@@ -486,8 +524,8 @@
 
 
 def final_kernel(
-    lines, piece, states, norm, pred, carried, glow, mid_terms, end_terms, owner,
-    alpha, beta, counts,
+    lines, piece, states, norm, pred_far, carried_far, emission, mid_far, end_far, owner,
+    alpha, beta, counts, pred, carried, glow, mid_terms, end_terms, load_sems,
     out_f, in_f, red_f, land_f, out_b, in_b, red_b, natural, land_b,
     sums, in_s, red_s, land_s, mine, in_c, *sems,
 ):
@@ -495,6 +533,16 @@
     net.greet()
     src, dst = lines["src"], lines["dst"]
     traces = pred.shape[0]
+    loads = fetch(
+        [
+            (carried_far, carried),
+            (pred_far, pred),
+            (emission.at[pl.ds((STEPS - 1) * traces, traces)], glow),
+            (mid_far, mid_terms),
+            (end_far, end_terms),
+        ],
+        load_sems,
+    )
     shape = (traces, LANES)
     number = net.place["dst"] * src + net.place["src"]
     to_src, to_dst = lax.div(number, dst), lax.rem(number, dst)
@@ -511,6 +559,8 @@
                 device_id_type=pl.DeviceIdType.MESH,
             )
 
+    for copy in loads:
+        copy.wait()
     terms = [mid_terms[0], end_terms[0], end_terms[1]]
     rows = [jnp.sum(pred[...] * glow[...], axis=1, keepdims=True)]
     rows.append(jnp.sum(carried[...], axis=1, keepdims=True))
@@ -593,11 +643,16 @@
         begin = pl.multiple_of(net.origin("src", k) * piece, piece)
         alpha[:, pl.ds(begin, piece)] = part * scale
     value = jnp.zeros(counts.shape, jnp.float32)
+    blocks = counts.shape[0]
+    wanted = net.place["src"] * blocks + lax.broadcasted_iota(
+        jnp.int32, (blocks, owner.shape[2]), 0
+    )
     for k in range(src):
         if k:
             third_c[k - 1].wait_recv()
+        owned = (owner[net.origin("src", k)] == wanted).astype(jnp.float32)
         value = value + jnp.dot(
-            owner[net.origin("src", k)], mine[...] if k == 0 else in_c[k],
+            owned, mine[...] if k == 0 else in_c[k],
             precision=lax.Precision.HIGHEST, preferred_element_type=jnp.float32,
         )
     counts[...] = value
@@ -647,10 +702,16 @@
     def f32(*shape):
         return jax.ShapeDtypeStruct(shape, jnp.float32)
 
+    def bf16(*shape):
+        return jax.ShapeDtypeStruct(shape, jnp.bfloat16)
+
     def room(*shape, dtype=jnp.float32):
         return pltpu.VMEM(shape, dtype)
 
     half = functools.partial(room, dtype=jnp.bfloat16)
+
+    def outside(array):
+        return pltpu.with_memory_space_constraint(array, pltpu.HBM)
 
     vocab_slice = word_table.shape[0]
     local_ids = tokens.reshape(-1) - dst_place * vocab_slice
@@ -659,19 +720,26 @@
     )
     looked = jnp.dot(onehot, word_table, preferred_element_type=jnp.float32)
     share = piece // dst_count
-    gathered, masks, emission, alpha_moved = pl.pallas_call(
-        functools.partial(gather_kernel, lines, group, piece, states),
+    gathered, masks, emission, last_weights, alpha_moved = pl.pallas_call(
+        functools.partial(gather_kernel, lines, group, piece),
         out_shape=(
-            half(dst_count, dst_count, share, emb_width),
+            pltpu.HBM((dst_count, dst_count, share, emb_width), jnp.bfloat16),
             jax.ShapeDtypeStruct((src_count,) + block_mask.shape, jnp.int32),
-            f32(STEPS * traces, col_count),
-            f32(traces, piece),
+            pltpu.HBM((STEPS * traces, col_count), jnp.float32),
+            pltpu.HBM((traces, col_count), jnp.bfloat16),
+            pltpu.HBM((traces, piece), jnp.float32),
         ),
-        in_specs=[hbm, vmem, vmem, vmem, vmem, hbm],
-        out_specs=(vmem,) * 4,
+        in_specs=[hbm, vmem, vmem, hbm, hbm, hbm, hbm],
+        out_specs=(hbm, vmem, hbm, hbm, hbm),
         scratch_shapes=[
             half(dst_count, STEPS * traces, emb_width),
+            half(col_count, emb_width),
+            room(1, col_count),
+            room(traces, col_count),
+            room(STEPS * traces, col_count),
+            half(traces, col_count),
             pltpu.SemaphoreType.DMA,
+            pltpu.SemaphoreType.DMA((3,)),
             pltpu.SemaphoreType.DMA((3,)),
         ]
         + [on_src, on_src, on_dst, on_dst, on_src, on_src]
@@ -681,14 +749,10 @@
         ),
         name="gather",
     )(
-        pltpu.with_memory_space_constraint(
-            src_emb.reshape(group, src_count, dst_count, share, emb_width), pltpu.HBM
-        ),
-        block_mask, looked.astype(jnp.bfloat16), out_emb, log_norm[None, :],
-        pltpu.with_memory_space_constraint(alpha_start, pltpu.HBM),
-    )
-    gathered = pltpu.with_memory_space_constraint(gathered, pltpu.VMEM)
-    emission = emission.reshape(STEPS, traces, col_count)
+        outside(src_emb.reshape(group, src_count, dst_count, share, emb_width)),
+        block_mask, looked.astype(jnp.bfloat16), outside(out_emb),
+        outside(log_norm[None, :]), outside(beta_end), outside(alpha_start),
+    )
     whole_mask = masks.reshape(src_count * block_mask.shape[0], cols)
     unit_index = jnp.arange(units, dtype=jnp.int32)
     per_piece = piece // unit
@@ -714,14 +778,19 @@
     top, mass, near, far = pl.pallas_call(
         functools.partial(table_kernel, unit, cols, held),
         out_shape=(
-            jax.ShapeDtypeStruct((cols, row_count), jnp.float32),
-            jax.ShapeDtypeStruct((cols, row_count), jnp.float32),
-            pltpu.VMEM((held, BLK, unit), jnp.bfloat16),
+            f32(cols, row_count),
+            f32(cols, row_count),
+            half(held, BLK, unit),
             jax.ShapeDtypeStruct((max(places - held, 1), BLK, unit), jnp.bfloat16),
         ),
-        in_specs=[smem, smem, vmem, vmem],
+        in_specs=[smem, smem, hbm, hbm],
         out_specs=(vmem, vmem, vmem, anywhere),
-        scratch_shapes=[pltpu.VMEM((BLK, unit), jnp.bfloat16)] * 2
+        scratch_shapes=[
+            half(dst_count, dst_count, share, emb_width),
+            half(col_count, emb_width),
+            pltpu.SemaphoreType.DMA((2,)),
+        ]
+        + [pltpu.VMEM((BLK, unit), jnp.bfloat16)] * 2
         + [pltpu.VMEM((BLK, unit), jnp.float32)] * 2
         + [pltpu.VMEM((1, unit), jnp.float32)] * 2
         + [pltpu.SemaphoreType.DMA((2,))],
@@ -732,7 +801,7 @@
             transcendentals=guess * BLK * unit,
         ),
         name="table",
-    )(ids, number, gathered, dst_emb)
+    )(ids, number, outside(gathered), outside(dst_emb))
     near = pltpu.with_memory_space_constraint(near, pltpu.VMEM)
 
     factor, alpha_rows = pl.pallas_call(
@@ -745,6 +814,7 @@
             room(dst_count, 1, piece),
             room(1, piece),
             room(dst_count, 1, piece),
+            half(traces, piece),
             half(dst_count, traces, piece),
         ]
         + [on_dst] * 6,
@@ -752,7 +822,7 @@
             collective_id=0, has_side_effects=True, vmem_limit_bytes=VMEM_BYTES
         ),
         name="stats",
-    )(top, mass, alpha_moved.astype(jnp.bfloat16), near)
+    )(top, mass, alpha_moved, near)
 
     lanes = -(-cols // LANES) * LANES
 
@@ -778,17 +848,19 @@
             name="sweep%d" % kind,
         )(ids, number, *alphas, factor, *weights, near, far)
 
-    def exchange(ahead, behind, glow, glow_next):
+    def exchange(ahead, behind, step, later):
         width = piece + LANES
         return pl.pallas_call(
-            functools.partial(exchange_kernel, lines, piece, states),
-            out_shape=(
-                f32(traces, row_count),
-                jax.ShapeDtypeStruct((traces, col_count), jnp.bfloat16),
-            ),
-            in_specs=[vmem] * 5,
+            functools.partial(exchange_kernel, lines, piece, states, step, later),
+            out_shape=(f32(traces, row_count), bf16(traces, col_count)),
+            in_specs=[hbm] * 3 + [vmem],
             out_specs=(vmem, vmem),
             scratch_shapes=[
+                room(traces, col_count),
+                room(traces, row_count),
+                room(traces, col_count),
+                room(traces, col_count),
+                pltpu.SemaphoreType.DMA((4,)),
                 half(src_count, traces, width),
                 half(dst_count, traces, width),
                 half(src_count, traces, width),
@@ -800,35 +872,38 @@
             ]
             + [on_src, on_dst, on_src, on_dst, on_dst, on_src, on_dst, on_src],
             compiler_params=pltpu.CompilerParams(
-                collective_id=1, has_side_effects=True, vmem_limit_bytes=VMEM_BYTES
+                collective_id=1 + 3 * step, has_side_effects=True, vmem_limit_bytes=VMEM_BYTES
             ),
             name="exchange",
-        )(ahead, behind, glow, glow_next, near)
-
-    last_weights = (emission[2] * beta_end).astype(jnp.bfloat16)
+        )(outside(ahead), outside(behind), outside(emission), near)
+
     pred, carried = sweep(0, [alpha_rows], [last_weights])
-    alpha_1, weights_2 = exchange(pred, carried, emission[0], emission[1])
+    alpha_1, weights_2 = exchange(pred, carried, 0, 1)
     pred, carried, middle_terms = sweep(1, [alpha_1], [weights_2])
-    alpha_2, weights_1 = exchange(pred, carried, emission[1], emission[0])
+    alpha_2, weights_1 = exchange(pred, carried, 1, 0)
     pred, carried, end_terms = sweep(2, [alpha_2, alpha_rows], [weights_1, last_weights])
 
     mask_rows = block_mask.shape[0]
-    all_state = (
-        (unit_index[None, :] // per_piece) * col_count
-        + jnp.arange(src_count, dtype=jnp.int32)[:, None] * piece
-        + (unit_index[None, :] % per_piece) * unit
-    )
-    row_block = src_place * mask_rows + jnp.arange(mask_rows, dtype=jnp.int32)
-    chosen = (all_state // BLK)[:, None, :] == row_block[None, :, None]
+    index = np.arange(units)
+    all_state = (index // per_piece * col_count + index % per_piece * unit)[None, :] + (
+        np.arange(src_count)[:, None] * piece
+    )
+    unit_blocks = jnp.asarray((all_state // BLK)[:, None, :], jnp.int32)
     norm = mask_rows * src_count * cols * dst_count / (STEPS * traces)
     alpha_end, beta_start, block_counts = pl.pallas_call(
         functools.partial(final_kernel, lines, piece, states, norm),
         out_shape=(
             f32(traces, col_count), f32(traces, row_count), f32(mask_rows, lanes),
         ),
-        in_specs=[vmem] * 6,
+        in_specs=[hbm] * 5 + [vmem],
         out_specs=(vmem,) * 3,
         scratch_shapes=[
+            room(traces, col_count),
+            room(traces, row_count),
+            room(traces, col_count),
+            room(1, units, traces, lanes),
+            room(2, units, traces, lanes),
+            pltpu.SemaphoreType.DMA((5,)),
             room(src_count, traces, piece),
             room(src_count, traces, piece),
             room(traces, piece),
@@ -851,7 +926,10 @@
             collective_id=2, has_side_effects=True, vmem_limit_bytes=VMEM_BYTES
         ),
         name="final",
-    )(pred, carried, emission[2], middle_terms, end_terms, chosen.astype(jnp.float32))
+    )(
+        outside(pred), outside(carried), outside(emission), outside(middle_terms),
+        outside(end_terms), unit_blocks,
+    )
     return (alpha_end, beta_start, block_counts[:, :cols])
 
 

time: 262 us -> 252 us (0.962)
  local copies, waits for them, and re-layouts: 13 us -> 3.47 us
    unnamed x26 -> x10, local copies, waits for them, and re-layouts: 12.8 us -> 3.25 us
    pallas_call x3, Pallas kernels: 78.5 us -> 84.1 us  [sweep(): pl.pallas_call(functools.partial(sweep_kernel, unit, cols, held, traces,...]
    pallas_call x1, Pallas kernels: 20.6 us -> 16.1 us  [local(): pl.pallas_call(functools.partial(stats_kernel, lines, piece), out_shape=(...]
    pallas_call x1, Pallas kernels: 44.7 us -> 48 us  [local(): pl.pallas_call(functools.partial(table_kernel, unit, cols, held), out_sha...]
where the time goes in v3:
time: 252 us
  Pallas kernels  244 us (97%)
  local copies, waits for them, and re-layouts  3.47 us (1%)
  other arithmetic  3.19 us (1%)
    pallas_call x3, Pallas kernels, sweep(): pl.pallas_call(functools.partial(sweep_kernel, unit, cols, held, traces,...  84.1 us
    pallas_call x1, Pallas kernels, local(): pl.pallas_call(functools.partial(table_kernel, unit, cols, held), out_sha...  48 us
    pallas_call x1, Pallas kernels, local(): pl.pallas_call(functools.partial(gather_kernel, lines, group, piece), out...  38 us
    pallas_call x1, Pallas kernels, local(): pl.pallas_call(functools.partial(final_kernel, lines, piece, states, norm...  29.6 us
    pallas_call x2, Pallas kernels, exchange(): pl.pallas_call(functools.partial(exchange_kernel, lines, piece, states, s...  28.2 us
    pallas_call x1, Pallas kernels, local(): pl.pallas_call(functools.partial(stats_kernel, lines, piece), out_shape=(...  16.1 us

profile of v3, /device:TPU:1, one launch (start us, length us, event | category | flops | bytes accessed | tf_op | source)
XLA Modules:
  0.0 251.7 jit_solution(16169194209866019456)
XLA Ops:
  0.6 0.0 copy-start
  0.7 0.8 broadcast_subtract_fusion
  1.4 0.1 sub.27
  1.5 0.1 iota_compare_fusion.4
  1.6 0.3 copy-done
  1.9 0.3 convolution_convert_fusion.looked
  2.2 0.8 copy.17.mask
  3.0 38.0 %gather.1 = (bf16[8,8,256,128]{3,2,1,0:T(8,128)(2,1)}, s32[4,32,16]{2,1,0:T(8,128)S(1)}, f32[24,8192]{1,0:T(8,128)}, bf16[8,8192]{1,0:T(8,128)(2,1)}, f32[8,2048]{1,0:T(8,128)}) custom-call(bf16[2,4,8,256,128]{4,3,2,1,0:T(8,128)(2,1)} %bitcast.8, s32[32,16]{1,0:T(8,128)S(1)} %copy.17.mask, bf16[24,128]{1,0:T(8,128)(2,1)S(1)} %convolution_convert_fusion.looked, ...), custom_call_target="tpu_custom_call" | custom-call | tf_op jit(solution)/shard_map/gather/pallas_call | solution.py:723
  41.0 0.1 copy.18
  41.1 0.6 select_reduce_fusion.2
  41.7 0.7 convert_reduce_fusion
  42.4 0.1 eq.66
  42.5 0.2 select_reduce_fusion.1
  42.6 0.9 select_reduce_fusion.ids
  43.5 48.0 %table.1 = (f32[16,16384]{1,0:T(8,128)}, f32[16,16384]{1,0:T(8,128)}, bf16[96,512,512]{2,1,0:T(8,128)(2,1)S(1)}, bf16[416,512,512]{2,1,0:T(8,128)(2,1)}) custom-call(s32[512]{0:T(512)} %select_reduce_fusion.ids, s32[1]{0:T(128)} %bitcast.3.count, bf16[8,8,256,128]{3,2,1,0:T(8,128)(2,1)} %get-tuple-element.30.src_far, bf16[8192,128]{1,0:T(8,128)(2,1)} %dst_far.1), custom_call_target="tpu_custom_call" | custom-call | flops 6912212992 | bytes 27000832 | tf_op jit(solution)/shard_map/table/pallas_call | solution.py:778
  91.5 16.1 %stats.1 = (f32[16,16384]{1,0:T(8,128)}, f32[8,16384]{1,0:T(8,128)}) custom-call(f32[16,16384]{1,0:T(8,128)} %get-tuple-element.31.top, f32[16,16384]{1,0:T(8,128)} %get-tuple-element.32.mass, f32[8,2048]{1,0:T(8,128)} %get-tuple-element.33.alpha, bf16[96,512,512]{2,1,0:T(8,128)(2,1)S(1)} %get-tuple-element.34.near.refs_3_.refs_5_), custom_call_target="tpu_custom_call" | custom-call | tf_op jit(solution)/shard_map/stats/pallas_call | solution.py:807
  107.6 26.6 %sweep0.1 = (f32[8,8192]{1,0:T(8,128)}, f32[8,16384]{1,0:T(8,128)}) custom-call(s32[512]{0:T(512)} %select_reduce_fusion.ids, s32[1]{0:T(128)} %bitcast.3.count, f32[8,16384]{1,0:T(8,128)} %get-tuple-element.35.refs_0_.refs_1_, f32[16,16384]{1,0:T(8,128)} %get-tuple-element.36.refs_1_.refs_2_, bf16[8,8192]{1,0:T(8,128)(2,1)} %get-tuple-element.37.refs_2_.refs_4_, ...), custom_call_target="tpu_custom_call" | custom-call | flops 864026624 | bytes 27000832 | tf_op jit(solution)/shard_map/sweep0/pallas_call | solution.py:833
  134.2 13.9 %exchange.2 = (f32[8,16384]{1,0:T(8,128)}, bf16[8,8192]{1,0:T(8,128)(2,1)}) custom-call(f32[8,8192]{1,0:T(8,128)} %get-tuple-element.39.pred_far, f32[8,16384]{1,0:T(8,128)} %get-tuple-element.40.carried_far, f32[24,8192]{1,0:T(8,128)} %get-tuple-element.41.emission, bf16[96,512,512]{2,1,0:T(8,128)(2,1)S(1)} %get-tuple-element.34.near.refs_3_.refs_5_), custom_call_target="tpu_custom_call" | custom-call | tf_op jit(solution)/shard_map/exchange/pallas_call | solution.py:853
  148.1 28.6 %sweep1.1 = (f32[8,8192]{1,0:T(8,128)}, f32[8,16384]{1,0:T(8,128)}, f32[1,32,8,128]{3,2,1,0:T(8,128)}) custom-call(s32[512]{0:T(512)} %select_reduce_fusion.ids, s32[1]{0:T(128)} %bitcast.3.count, f32[8,16384]{1,0:T(8,128)} %get-tuple-element.42.refs_0_, f32[16,16384]{1,0:T(8,128)} %get-tuple-element.36.refs_1_.refs_2_, ...), custom_call_target="tpu_custom_call" | custom-call | flops 864026624 | bytes 27000832 | tf_op jit(solution)/shard_map/sweep1/pallas_call | solution.py:833
  176.7 14.3 %exchange.3 = (f32[8,16384]{1,0:T(8,128)}, bf16[8,8192]{1,0:T(8,128)(2,1)}) custom-call(f32[8,8192]{1,0:T(8,128)} %get-tuple-element.44.pred_far, f32[8,16384]{1,0:T(8,128)} %get-tuple-element.45.carried_far, f32[24,8192]{1,0:T(8,128)} %get-tuple-element.41.emission, bf16[96,512,512]{2,1,0:T(8,128)(2,1)S(1)} %get-tuple-element.34.near.refs_3_.refs_5_), custom_call_target="tpu_custom_call" | custom-call | tf_op jit(solution)/shard_map/exchange/pallas_call | solution.py:853
  191.0 0.0 copy-start.2
  191.1 0.0 copy-start.1
  191.1 28.9 %sweep2.1 = (f32[8,8192]{1,0:T(8,128)}, f32[8,16384]{1,0:T(8,128)}, f32[2,32,8,128]{3,2,1,0:T(8,128)}) custom-call(s32[512]{0:T(512)} %select_reduce_fusion.ids, s32[1]{0:T(128)} %bitcast.3.count, f32[8,16384]{1,0:T(8,128)} %get-tuple-element.46.refs_0_, f32[8,16384]{1,0:T(8,128)} %get-tuple-element.35.refs_0_.refs_1_, ...), custom_call_target="tpu_custom_call" | custom-call | flops 864026624 | bytes 27000832 | tf_op jit(solution)/shard_map/sweep2/pallas_call | solution.py:833
  220.0 0.0 copy-done.2
  220.0 29.6 %final.1 = (f32[8,8192]{1,0:T(8,128)S(1)}, f32[8,16384]{1,0:T(8,128)S(1)}, f32[32,128]{1,0:T(8,128)S(1)}) custom-call(f32[8,8192]{1,0:T(8,128)} %get-tuple-element.48.pred_far, f32[8,16384]{1,0:T(8,128)} %get-tuple-element.49.carried_far, f32[24,8192]{1,0:T(8,128)} %get-tuple-element.41.emission, f32[1,32,8,128]{3,2,1,0:T(8,128)} %get-tuple-element.50.mid_far, ...), custom_call_target="tpu_custom_call" | custom-call | tf_op jit(solution)/shard_map/final/pallas_call | solution.py:893
  249.5 0.7 copy.19
  250.2 0.7 copy.22
  250.9 0.8 copy.23
  251.7 0.0 copy-done.1
  (1 shorter events, 0.0 us)
Async XLA Ops:
  0.6 1.2 copy-start
  191.0 28.9 %copy-start.2 = (s32[4,1,32]{2,1,0:T(1,128)S(1)}, s32[4,1,32]{2,1,0:T(1,128)}, u32[]{:S(2)}) copy-start(s32[4,1,32]{2,1,0:T(1,128)} %constant.63.clone.owner) | copy-start | bytes 1540
  191.1 60.7 %copy-start.1 = (bf16[4096,128]{1,0:T(8,128)(2,1)S(1)}, bf16[4096,128]{1,0:T(8,128)(2,1)}, u32[]{:S(2)}) copy-start(bf16[4096,128]{1,0:T(8,128)(2,1)} %param.13) | copy-start | bytes 3145732

commit v4 on v3

--- a/solution.py
+++ b/solution.py
@@ -260,7 +260,7 @@
 
 def gather_kernel(
     lines, group, piece, source, mask, looked, out_far, norm_far, end_far, start,
-    rows, masks, emission_far, last_far, moved, land_w, out_emb, log_norm, end, emission, last,
+    rows_far, masks, emission_far, last_far, moved, rows, land_w, out_emb, log_norm, end, emission, last,
     local_sems, alpha_sems, load_sems, *sems,
 ):
     net = Lines(lines)
@@ -302,8 +302,11 @@
         copy.start()
         return copy
 
+    order = sorted(range(1, src), key=lambda k: min(k, src - k))
     along = []
-    for k in range(1, src):
+
+    def next_round():
+        k = order[len(along)]
         other = net.peer("src", k)
         along.append(
             pass_on(
@@ -311,6 +314,8 @@
                 sems[0].at[k], sems[1].at[k], {"src": other},
             )
         )
+
+    next_round()
     words = net.send("dst", lambda peer: looked, land_w, sems[2], sems[3])
     masks[z] = mask[...]
     marks = [
@@ -333,12 +338,14 @@
     def _():
         stay.start()
 
-    own = pltpu.make_async_copy(source.at[:, z], rows.at[plane(z)], local_sems)
+    own = pltpu.make_async_copy(source.at[:, z], rows_far.at[plane(z)], local_sems.at[0])
     own.start()
 
     across, beside = [], []
-    for k in range(1, src):
-        along[k - 1].wait_recv()
+    for n, k in enumerate(order):
+        along[n].wait_recv()
+        if n + 1 < len(order):
+            next_round()
         here = plane(net.origin("src", k))
         block = rows.at[here, d]
         for m in range(1, chips):
@@ -351,7 +358,7 @@
         beside.append(
             pass_on(block, block, sems[8].at[k, 0], sems[9].at[k, 0], {"dst": sibling})
         )
-        if k == 1:
+        if n == 0:
             total = looked[...].astype(jnp.float32)
             for w in range(1, dst):
                 words[w - 1].wait_recv()
@@ -371,15 +378,24 @@
                 tail = risen[risen.shape[0] - end.shape[0]:]
                 last[:, c:c + width] = (tail * end[:, c:c + width]).astype(jnp.bfloat16)
             stores = fetch([(emission, emission_far), (last, last_far)], load_sems)
-    for k in range(1, src):
+    for n, k in enumerate(order):
         here = plane(net.origin("src", k))
         for m in range(1, chips):
-            across[(k - 1) * (chips - 1) + m - 1].wait_recv()
+            across[n * (chips - 1) + m - 1].wait_recv()
             block = rows.at[here, lax.rem(d + dst - 2 * m, dst)]
             beside.append(
                 pass_on(block, block, sems[8].at[k, m], sems[9].at[k, m], {"dst": sibling})
             )
-    own.wait()
+    out = [own]
+    for n, k in enumerate(order):
+        here = plane(net.origin("src", k))
+        beside[n].wait_recv()
+        first = len(order) + n * (chips - 1)
+        for copy in beside[first:first + chips - 1]:
+            copy.wait_recv()
+        copy = pltpu.make_async_copy(rows.at[here], rows_far.at[here], local_sems.at[n + 1])
+        copy.start()
+        out.append(copy)
     for copy in stores:
         copy.wait()
     for copy in marks:
@@ -394,8 +410,8 @@
     def _():
         stay.wait()
 
-    for copy in beside:
-        copy.wait_recv()
+    for copy in out:
+        copy.wait()
     for copies in (along, words, marks, across, beside):
         for copy in copies:
             copy.wait_send()
@@ -592,14 +608,6 @@
     red_s[...] = total
     second_s = net.send("dst", lambda peer: red_s, land_s, sems[6], sems[7])
 
-    value = out_f[net.place["src"]]
-    for k in range(1, src):
-        first_f[k - 1].wait_recv()
-        value = value + in_f[k]
-    start = pl.multiple_of(net.place["src"] * piece, piece)
-    red_f[...] = value * glow[:, pl.ds(start, piece)]
-    second_f = net.send("src", lambda peer: red_f, land_f, sems[8], sems[9])
-
     value = out_b[net.place["dst"]]
     for k in range(1, dst):
         first_b[k - 1].wait_recv()
@@ -614,6 +622,12 @@
     def _():
         move.start()
 
+    value = out_f[net.place["src"]]
+    for k in range(1, src):
+        first_f[k - 1].wait_recv()
+        value = value + in_f[k]
+    start = pl.multiple_of(net.place["src"] * piece, piece)
+    red_f[...] = value * glow[:, pl.ds(start, piece)]
     total = red_s[...]
     for k in range(1, dst):
         second_s[k - 1].wait_recv()
@@ -634,6 +648,7 @@
         natural[...] = red_b[...]
 
     third_b = net.send("dst", lambda peer: natural, land_b, sems[13], sems[14])
+    second_f = net.send("src", lambda peer: red_f, land_f, sems[8], sems[9])
 
     scale = states / total[0][:, :1]
     for k in range(src):
@@ -732,13 +747,14 @@
         in_specs=[hbm, vmem, vmem, hbm, hbm, hbm, hbm],
         out_specs=(hbm, vmem, hbm, hbm, hbm),
         scratch_shapes=[
+            half(dst_count, dst_count, share, emb_width),
             half(dst_count, STEPS * traces, emb_width),
             half(col_count, emb_width),
             room(1, col_count),
             room(traces, col_count),
             room(STEPS * traces, col_count),
             half(traces, col_count),
-            pltpu.SemaphoreType.DMA,
+            on_src,
             pltpu.SemaphoreType.DMA((3,)),
             pltpu.SemaphoreType.DMA((3,)),
         ]

time: 252 us -> 250 us (level)
  Pallas kernels: 244 us -> 241 us
    pallas_call x1, Pallas kernels: 29.6 us -> 25.6 us  [local(): pl.pallas_call(functools.partial(final_kernel, lines, piece, states, norm...]
    pallas_call x1, Pallas kernels: 16.1 us -> 19.5 us  [local(): pl.pallas_call(functools.partial(stats_kernel, lines, piece), out_shape=(...]
    pallas_call x3, Pallas kernels: 84.1 us -> 81.1 us  [sweep(): pl.pallas_call(functools.partial(sweep_kernel, unit, cols, held, traces,...]
where the time goes in v4:
time: 250 us; the launch traced here: 249 us
  Pallas kernels  241 us (96%)
  local copies, waits for them, and re-layouts  3.47 us (1%)
  other arithmetic  3.19 us (1%)
    pallas_call x3, Pallas kernels, sweep(): pl.pallas_call(functools.partial(sweep_kernel, unit, cols, held, traces,...  81.1 us
    pallas_call x1, Pallas kernels, local(): pl.pallas_call(functools.partial(table_kernel, unit, cols, held), out_sha...  46.7 us
    pallas_call x1, Pallas kernels, local(): pl.pallas_call(functools.partial(gather_kernel, lines, group, piece), out...  38 us
    pallas_call x2, Pallas kernels, exchange(): pl.pallas_call(functools.partial(exchange_kernel, lines, piece, states, s...  30.6 us
    pallas_call x1, Pallas kernels, local(): pl.pallas_call(functools.partial(final_kernel, lines, piece, states, norm...  25.6 us
    pallas_call x1, Pallas kernels, local(): pl.pallas_call(functools.partial(stats_kernel, lines, piece), out_shape=(...  19.5 us

profile of v4, /device:TPU:1, one launch (start us, length us, event | category | flops | bytes accessed | tf_op | source)
XLA Modules:
  0.0 249.2 jit_solution(15867135729364696566)
XLA Ops:
  0.6 0.0 copy-start
  0.7 0.8 broadcast_subtract_fusion
  1.4 0.1 sub.27
  1.5 0.1 iota_compare_fusion.4
  1.6 0.3 copy-done
  1.9 0.3 convolution_convert_fusion.looked
  2.2 0.8 copy.17.mask
  3.0 38.0 %gather.1 = (bf16[8,8,256,128]{3,2,1,0:T(8,128)(2,1)}, s32[4,32,16]{2,1,0:T(8,128)S(1)}, f32[24,8192]{1,0:T(8,128)}, bf16[8,8192]{1,0:T(8,128)(2,1)}, f32[8,2048]{1,0:T(8,128)}) custom-call(bf16[2,4,8,256,128]{4,3,2,1,0:T(8,128)(2,1)} %bitcast.8, s32[32,16]{1,0:T(8,128)S(1)} %copy.17.mask, bf16[24,128]{1,0:T(8,128)(2,1)S(1)} %convolution_convert_fusion.looked, ...), custom_call_target="tpu_custom_call" | custom-call | tf_op jit(solution)/shard_map/gather/pallas_call | solution.py:738
  41.0 0.1 copy.18
  41.1 0.6 select_reduce_fusion.2
  41.7 0.7 convert_reduce_fusion
  42.4 0.1 eq.66
  42.5 0.2 select_reduce_fusion.1
  42.6 0.9 select_reduce_fusion.ids
  43.5 46.7 %table.1 = (f32[16,16384]{1,0:T(8,128)}, f32[16,16384]{1,0:T(8,128)}, bf16[96,512,512]{2,1,0:T(8,128)(2,1)S(1)}, bf16[416,512,512]{2,1,0:T(8,128)(2,1)}) custom-call(s32[512]{0:T(512)} %select_reduce_fusion.ids, s32[1]{0:T(128)} %bitcast.3.count, bf16[8,8,256,128]{3,2,1,0:T(8,128)(2,1)} %get-tuple-element.30.src_far, bf16[8192,128]{1,0:T(8,128)(2,1)} %dst_far.1), custom_call_target="tpu_custom_call" | custom-call | flops 6912212992 | bytes 27000832 | tf_op jit(solution)/shard_map/table/pallas_call | solution.py:794
  90.2 19.5 %stats.1 = (f32[16,16384]{1,0:T(8,128)}, f32[8,16384]{1,0:T(8,128)}) custom-call(f32[16,16384]{1,0:T(8,128)} %get-tuple-element.31.top, f32[16,16384]{1,0:T(8,128)} %get-tuple-element.32.mass, f32[8,2048]{1,0:T(8,128)} %get-tuple-element.33.alpha, bf16[96,512,512]{2,1,0:T(8,128)(2,1)S(1)} %get-tuple-element.34.near.refs_3_.refs_5_), custom_call_target="tpu_custom_call" | custom-call | tf_op jit(solution)/shard_map/stats/pallas_call | solution.py:823
  109.7 25.6 %sweep0.1 = (f32[8,8192]{1,0:T(8,128)}, f32[8,16384]{1,0:T(8,128)}) custom-call(s32[512]{0:T(512)} %select_reduce_fusion.ids, s32[1]{0:T(128)} %bitcast.3.count, f32[8,16384]{1,0:T(8,128)} %get-tuple-element.35.refs_0_.refs_1_, f32[16,16384]{1,0:T(8,128)} %get-tuple-element.36.refs_1_.refs_2_, bf16[8,8192]{1,0:T(8,128)(2,1)} %get-tuple-element.37.refs_2_.refs_4_, ...), custom_call_target="tpu_custom_call" | custom-call | flops 864026624 | bytes 27000832 | tf_op jit(solution)/shard_map/sweep0/pallas_call | solution.py:849
  135.3 15.0 %exchange.2 = (f32[8,16384]{1,0:T(8,128)}, bf16[8,8192]{1,0:T(8,128)(2,1)}) custom-call(f32[8,8192]{1,0:T(8,128)} %get-tuple-element.39.pred_far, f32[8,16384]{1,0:T(8,128)} %get-tuple-element.40.carried_far, f32[24,8192]{1,0:T(8,128)} %get-tuple-element.41.emission, bf16[96,512,512]{2,1,0:T(8,128)(2,1)S(1)} %get-tuple-element.34.near.refs_3_.refs_5_), custom_call_target="tpu_custom_call" | custom-call | tf_op jit(solution)/shard_map/exchange/pallas_call | solution.py:869
  150.3 27.6 %sweep1.1 = (f32[8,8192]{1,0:T(8,128)}, f32[8,16384]{1,0:T(8,128)}, f32[1,32,8,128]{3,2,1,0:T(8,128)}) custom-call(s32[512]{0:T(512)} %select_reduce_fusion.ids, s32[1]{0:T(128)} %bitcast.3.count, f32[8,16384]{1,0:T(8,128)} %get-tuple-element.42.refs_0_, f32[16,16384]{1,0:T(8,128)} %get-tuple-element.36.refs_1_.refs_2_, ...), custom_call_target="tpu_custom_call" | custom-call | flops 864026624 | bytes 27000832 | tf_op jit(solution)/shard_map/sweep1/pallas_call | solution.py:849
  177.9 15.6 %exchange.3 = (f32[8,16384]{1,0:T(8,128)}, bf16[8,8192]{1,0:T(8,128)(2,1)}) custom-call(f32[8,8192]{1,0:T(8,128)} %get-tuple-element.44.pred_far, f32[8,16384]{1,0:T(8,128)} %get-tuple-element.45.carried_far, f32[24,8192]{1,0:T(8,128)} %get-tuple-element.41.emission, bf16[96,512,512]{2,1,0:T(8,128)(2,1)S(1)} %get-tuple-element.34.near.refs_3_.refs_5_), custom_call_target="tpu_custom_call" | custom-call | tf_op jit(solution)/shard_map/exchange/pallas_call | solution.py:869
  193.5 0.0 copy-start.2
  193.5 0.0 copy-start.1
  193.6 27.9 %sweep2.1 = (f32[8,8192]{1,0:T(8,128)}, f32[8,16384]{1,0:T(8,128)}, f32[2,32,8,128]{3,2,1,0:T(8,128)}) custom-call(s32[512]{0:T(512)} %select_reduce_fusion.ids, s32[1]{0:T(128)} %bitcast.3.count, f32[8,16384]{1,0:T(8,128)} %get-tuple-element.46.refs_0_, f32[8,16384]{1,0:T(8,128)} %get-tuple-element.35.refs_0_.refs_1_, ...), custom_call_target="tpu_custom_call" | custom-call | flops 864026624 | bytes 27000832 | tf_op jit(solution)/shard_map/sweep2/pallas_call | solution.py:849
  221.4 0.0 copy-done.2
  221.4 25.6 %final.1 = (f32[8,8192]{1,0:T(8,128)S(1)}, f32[8,16384]{1,0:T(8,128)S(1)}, f32[32,128]{1,0:T(8,128)S(1)}) custom-call(f32[8,8192]{1,0:T(8,128)} %get-tuple-element.48.pred_far, f32[8,16384]{1,0:T(8,128)} %get-tuple-element.49.carried_far, f32[24,8192]{1,0:T(8,128)} %get-tuple-element.41.emission, f32[1,32,8,128]{3,2,1,0:T(8,128)} %get-tuple-element.50.mid_far, ...), custom_call_target="tpu_custom_call" | custom-call | tf_op jit(solution)/shard_map/final/pallas_call | solution.py:909
  247.0 0.7 copy.19
  247.7 0.7 copy.22
  248.4 0.8 copy.23
  249.2 0.0 copy-done.1
  (1 shorter events, 0.0 us)
Async XLA Ops:
  0.6 1.2 copy-start
  193.5 27.9 %copy-start.2 = (s32[4,1,32]{2,1,0:T(1,128)S(1)}, s32[4,1,32]{2,1,0:T(1,128)}, u32[]{:S(2)}) copy-start(s32[4,1,32]{2,1,0:T(1,128)} %constant.63.clone.owner) | copy-start | bytes 1540
  193.5 55.7 %copy-start.1 = (bf16[4096,128]{1,0:T(8,128)(2,1)S(1)}, bf16[4096,128]{1,0:T(8,128)(2,1)}, u32[]{:S(2)}) copy-start(bf16[4096,128]{1,0:T(8,128)(2,1)} %param.13) | copy-start | bytes 3145732
